TPU v7x, 128 devices: a whole 4x4x4 slice. The times are simulated.
128 devices in a mesh: aux: 128 (over y, x, z, core).
Axes of the slice: x: 4, y: 4, z: 4, core: 2. Of those that a mesh axis runs over, the one named last changes fastest.
Arguments:
- state: float32 [128, 2, 256, 256], P('aux'), may hold values from -6 to 6
- h_static: float32 [2, 256, 256], replicated, may hold values from -0.375 to 0.375
- drive_op: float32 [2, 256, 256], replicated, may hold values from -0.375 to 0.375
- couple: float32 [3, 256, 256], replicated, may hold values from -0.375 to 0.375
- bath_coef: float32 [2, 3], replicated, may hold values from -2 to 2
- damping: float32 [3], replicated, may hold values from 0.3 to 3
- occupation: int32 [128, 3], P('aux'), may hold values from 1 to 3
- raise_nbr: int32 [128, 3], P('aux'), may hold values from -1 to 127, as said below
- lower_nbr: int32 [128, 3], P('aux'), may hold values from -1 to 127, as said below
Outputs:
- new_state: float32 [128, 2, 256, 256], P('aux')
Inputs may be any that keep to these rules, and one draw needn't show every extreme that they name: `raise_nbr`: each entry is -1 or the index of an auxiliary matrix held on a device 1 to 2 after its own holder (auxiliary a is held by device a); the first mode's entry is -1 only on the last 2 devices. `lower_nbr`: each entry is -1 or the index of an auxiliary matrix held on a device 1 to 2 before its own holder (auxiliary a is held by device a); the first mode's entry is -1 only on the first 2 devices.
All inputs are finite; a program needn't handle non-finite values.
Results may differ from a plain program's by a relative error of at most 0.0003.
Values sent between devices are 32-bit elements; how exact they have to be, the bound alone decides.
A program may use at most 64 MiB of HBM per device.

v0:
```python
import functools

import jax
import jax.numpy as jnp
import numpy as np
from jax import lax
from jax.experimental import pallas as pl
from jax.experimental.pallas import tpu as pltpu
from jax.sharding import PartitionSpec as P

MESH = pl.DeviceIdType.MESH
STEP = 0.05
AMP = 2.0
FREQ = 20.0
M = 256
MODES = 3
STAGES = 4
SIB, FAR, NEAR, BACK, OWN = range(5)
RE, IM = 0, 1
BF = jnp.bfloat16
F32 = jnp.float32


def split(value):
    high = value.astype(BF)
    return high, (value - high.astype(F32)).astype(BF)


def kernel(
    count,
    bath,
    damp,
    occ,
    up,
    down,
    state,
    h_static,
    drive_op,
    couple,
    out,
    ybuf,
    win,
    raw,
    herm,
    left_of,
    right_of,
    total,
    acc,
    load_sem,
    send_sem,
    recv_sem,
):
    me = lax.axis_index("aux")
    odd = lax.rem(me, 2)
    d = 1 - 2 * odd

    def at(offset):
        return lax.rem(me + offset + count, count)

    partner = [at(d), at(2 * d), at(-d), at(-2 * d)]

    loads = [
        pltpu.make_async_copy(state.at[0], ybuf.at[0], load_sem.at[0]),
        pltpu.make_async_copy(couple, raw.at[pl.ds(0, 3)], load_sem.at[1]),
        pltpu.make_async_copy(h_static, raw.at[pl.ds(3, 2)], load_sem.at[2]),
        pltpu.make_async_copy(drive_op, raw.at[pl.ds(5, 2)], load_sem.at[3]),
    ]
    for load in loads:
        load.start()

    barrier = pltpu.get_barrier_semaphore()
    for other in partner:
        pl.semaphore_signal(barrier, inc=1, device_id=(other,), device_id_type=MESH)
    pl.semaphore_wait(barrier, 4)

    def remote(src, stage, to_slot, plane, number, device):
        return pltpu.make_async_remote_copy(
            src_ref=src,
            dst_ref=win.at[stage, to_slot, plane],
            send_sem=send_sem.at[stage, number],
            recv_sem=recv_sem.at[stage, to_slot, plane],
            device_id=(device,),
            device_id_type=MESH,
        )

    def own_sends(stage):
        own = ybuf.at[stage]
        return [
            remote(own.at[RE], stage, FAR, RE, 0, partner[BACK]),
            remote(own.at[IM], stage, NEAR, IM, 1, partner[NEAR]),
            remote(own.at[RE], stage, BACK, RE, 2, partner[FAR]),
            remote(own.at[IM], stage, BACK, IM, 3, partner[FAR]),
            remote(own.at[RE], stage, SIB, RE, 4, partner[SIB]),
            remote(own.at[IM], stage, SIB, IM, 5, partner[SIB]),
        ]

    def forwards(stage):
        return [
            remote(win.at[stage, FAR, RE], stage, NEAR, RE, 6, partner[SIB]),
            remote(win.at[stage, NEAR, IM], stage, FAR, IM, 7, partner[SIB]),
        ]

    def arrived(stage, slot, plane):
        remote(
            win.at[stage, slot, plane], stage, slot, plane, 0, partner[SIB]
        ).wait_recv()

    loads[0].wait()
    for copy in own_sends(0):
        copy.start()

    for load in loads[1:]:
        load.wait()

    def put(slot, real, imag, imag_right):
        for row, value in ((0, real), (M, imag)):
            high, low = split(value)
            left_of[slot, pl.ds(row, M), pl.ds(0, M)] = high
            left_of[slot, pl.ds(row, M), pl.ds(M, M)] = low
            left_of[slot, pl.ds(row, M), pl.ds(2 * M, M)] = high
        for column, value in ((0, real), (M, imag_right)):
            high, low = split(value)
            right_of[slot, pl.ds(0, M), pl.ds(column, M)] = high
            right_of[slot, pl.ds(M, M), pl.ds(column, M)] = low
            right_of[slot, pl.ds(2 * M, M), pl.ds(column, M)] = high

    for k in range(MODES):
        value = raw[k]
        raw[k] = (value + value.T) * 0.5
    for k in range(2):
        value = raw[3 + 2 * k]
        herm[k, 0] = (value + value.T) * 0.5
        value = raw[4 + 2 * k]
        herm[k, 1] = (value - value.T) * 0.5

    rate = jnp.float32(0.0)
    for k in range(MODES):
        rate = rate + occ[0, k].astype(F32) * damp[k]

    for slot in range(4):
        real = jnp.zeros((M, M), F32)
        imag = jnp.zeros((M, M), F32)
        for k in range(MODES):
            raises = jnp.where(up[0, k] == partner[slot], 1.0, 0.0).astype(F32)
            lowers = jnp.where(
                down[0, k] == partner[slot], occ[0, k].astype(F32), 0.0
            ).astype(F32)
            real = real + (raises + lowers * bath[0, k]) * raw[k]
            imag = imag + (lowers * bath[1, k]) * raw[k]
        put(slot, real, imag, imag)

    acc[...] = jnp.zeros_like(acc)

    def add(slot, plane, value):
        high, low = split(value)
        left = jnp.dot(
            left_of[slot],
            jnp.concatenate([high, high, low], axis=0),
            preferred_element_type=F32,
        )
        right = jnp.dot(
            jnp.concatenate([high, high, low], axis=1),
            right_of[slot],
            preferred_element_type=F32,
        )
        minus = left[:M] - right[:, :M]
        plus = left[M:] + right[:, M:]
        if plane == RE:
            return minus, plus
        return -plus, minus

    drive = [np.float32(AMP) * np.cos(np.float32(FREQ * t)) for t in (0.0, STEP / 2, STEP)]

    def stage_body(stage, carry):
        now = jnp.where(
            stage == 0, drive[0], jnp.where(stage == STAGES - 1, drive[2], drive[1])
        ).astype(F32)
        real = herm[0, 0] + now * herm[1, 0]
        imag = herm[0, 1] + now * herm[1, 1]
        put(OWN, real, imag, -imag)

        for plane in (RE, IM):
            first, second = add(OWN, plane, ybuf[stage, plane])
            if plane == RE:
                total[0] = first
                total[1] = second
            else:
                total[0] += first
                total[1] += second

        def take(slot, plane):
            first, second = add(slot, plane, win[stage, slot, plane])
            total[0] += first
            total[1] += second

        hand = forwards(stage)
        arrived(stage, SIB, RE)
        take(SIB, RE)
        arrived(stage, SIB, IM)
        take(SIB, IM)
        arrived(stage, FAR, RE)
        hand[0].start()
        take(FAR, RE)
        arrived(stage, NEAR, IM)
        hand[1].start()
        take(NEAR, IM)
        arrived(stage, BACK, RE)
        take(BACK, RE)
        arrived(stage, NEAR, RE)
        take(NEAR, RE)
        arrived(stage, FAR, IM)
        take(FAR, IM)
        arrived(stage, BACK, IM)
        take(BACK, IM)

        weight = jnp.where((stage == 0) | (stage == STAGES - 1), 1.0, 2.0).astype(F32)
        ahead = jnp.where(stage == 2, STEP, STEP / 2).astype(F32)
        slope_re = total[1] - rate * ybuf[stage, RE]
        slope_im = -total[0] - rate * ybuf[stage, IM]

        @pl.when(stage < STAGES - 1)
        def _():
            ybuf[stage + 1, RE] = ybuf[0, RE] + ahead * slope_re
            ybuf[stage + 1, IM] = ybuf[0, IM] + ahead * slope_im
            for copy in own_sends(stage + 1):
                copy.start()

        acc[RE] += weight * slope_re
        acc[IM] += weight * slope_im
        return carry

    lax.fori_loop(0, STAGES, stage_body, 0)

    out[0] = ybuf[0] + (STEP / 6) * acc[...]

    def drain(stage, carry):
        for copy in own_sends(stage) + forwards(stage):
            copy.wait_send()
        return carry

    lax.fori_loop(0, STAGES, drain, 0)


def on_device(
    state, h_static, drive_op, couple, bath_coef, damping, occupation, raise_nbr, lower_nbr
):
    count = lax.axis_size("aux")
    smem = pl.BlockSpec(memory_space=pltpu.SMEM)
    anywhere = pl.BlockSpec(memory_space=pl.ANY)
    return pl.pallas_call(
        functools.partial(kernel, count),
        out_shape=jax.ShapeDtypeStruct(state.shape, F32),
        in_specs=[smem] * 5 + [anywhere] * 4,
        out_specs=pl.BlockSpec(memory_space=pltpu.VMEM),
        scratch_shapes=[
            pltpu.VMEM((STAGES, 2, M, M), F32),
            pltpu.VMEM((STAGES, 4, 2, M, M), F32),
            pltpu.VMEM((7, M, M), F32),
            pltpu.VMEM((2, 2, M, M), F32),
            pltpu.VMEM((5, 2 * M, 3 * M), BF),
            pltpu.VMEM((5, 3 * M, 2 * M), BF),
            pltpu.VMEM((2, M, M), F32),
            pltpu.VMEM((2, M, M), F32),
            pltpu.SemaphoreType.DMA((4,)),
            pltpu.SemaphoreType.DMA((STAGES, 8)),
            pltpu.SemaphoreType.DMA((STAGES, 4, 2)),
        ],
        compiler_params=pltpu.CompilerParams(
            collective_id=0, has_side_effects=True, vmem_limit_bytes=48 << 20
        ),
        name="rk_step",
    )(
        bath_coef,
        damping,
        occupation,
        raise_nbr,
        lower_nbr,
        state,
        h_static,
        drive_op,
        couple,
    )


def solution(mesh):
    return jax.shard_map(
        on_device,
        mesh=mesh,
        in_specs=(
            P("aux", None, None, None),
            P(),
            P(),
            P(),
            P(),
            P(),
            P("aux", None),
            P("aux", None),
            P("aux", None),
        ),
        out_specs=P("aux", None, None, None),
        check_vma=False,
    )
```

profile of v0, /device:TPU:1, one launch (start us, length us, event | category | flops | bytes accessed | tf_op | source)
XLA Modules:
  0.0 95.8 jit_solution(11568766948675896176)
XLA Ops:
  0.0 0.0 copy-start
  0.0 1.1 %copy-done = f32[3,256,256]{2,1,0:T(8,128)S(1)} copy-done((f32[3,256,256]{2,1,0:T(8,128)S(1)}, f32[3,256,256]{2,1,0:T(8,128)}, u32[]{:S(2)}) %copy-start) | copy-done | bytes 786456
  1.1 0.0 copy-start.1
  1.1 1.0 %copy-done.1 = f32[1,2,256,256]{3,2,1,0:T(8,128)S(1)} copy-done((f32[1,2,256,256]{3,2,1,0:T(8,128)S(1)}, f32[1,2,256,256]{3,2,1,0:T(8,128)}, u32[]{:S(2)}) %copy-start.1) | copy-done | bytes 524312
  2.2 0.0 copy-start.2
  2.2 1.0 %copy-done.2 = f32[2,256,256]{2,1,0:T(8,128)S(1)} copy-done((f32[2,256,256]{2,1,0:T(8,128)S(1)}, f32[2,256,256]{2,1,0:T(8,128)}, u32[]{:S(2)}) %copy-start.2) | copy-done | bytes 524312
  3.2 0.0 copy-start.3
  3.2 1.0 %copy-done.3 = f32[2,256,256]{2,1,0:T(8,128)S(1)} copy-done((f32[2,256,256]{2,1,0:T(8,128)S(1)}, f32[2,256,256]{2,1,0:T(8,128)}, u32[]{:S(2)}) %copy-start.3) | copy-done | bytes 524312
  4.3 0.0 copy-start.4
  4.3 0.7 copy-done.4
  4.9 0.0 copy-start.5
  4.9 0.7 copy-done.5
  5.6 0.0 copy-start.6
  5.6 0.7 copy-done.6
  6.3 0.0 copy-start.7
  6.3 0.7 copy-done.7
  6.9 0.0 copy-start.8
  6.9 0.7 copy-done.8
  7.6 87.4 %rk_step.1 = f32[1,2,256,256]{3,2,1,0:T(8,128)S(1)} custom-call(f32[2,3]{1,0:T(2,128)S(1)} %copy-done.4, f32[3]{0:T(128)S(1)} %copy-done.5, s32[1,3]{1,0:T(1,128)S(1)} %copy-done.6, s32[1,3]{1,0:T(1,128)S(1)} %copy-done.7, s32[1,3]{1,0:T(1,128)S(1)} %copy-done.8, f32[1,2,256,256]{3,2,1,0:T(8,128)S(1)} %copy-done.1, f32[2,256,256]{2,1,0:T(8,128)S(1)} %copy-done.2, ...), custom_call_target="tpu_custom_call" | custom-call | tf_op jit(solution)/shard_map/rk_step/pallas_call | solution.py:250
  95.0 0.8 copy.11
Async XLA Ops:
  0.0 1.1 %copy-start = (f32[3,256,256]{2,1,0:T(8,128)S(1)}, f32[3,256,256]{2,1,0:T(8,128)}, u32[]{:S(2)}) copy-start(f32[3,256,256]{2,1,0:T(8,128)} %couple.1) | copy-start | bytes 2359300
  1.1 1.0 %copy-start.1 = (f32[1,2,256,256]{3,2,1,0:T(8,128)S(1)}, f32[1,2,256,256]{3,2,1,0:T(8,128)}, u32[]{:S(2)}) copy-start(f32[1,2,256,256]{3,2,1,0:T(8,128)} %state.1) | copy-start | bytes 1572868
  2.2 1.0 %copy-start.2 = (f32[2,256,256]{2,1,0:T(8,128)S(1)}, f32[2,256,256]{2,1,0:T(8,128)}, u32[]{:S(2)}) copy-start(f32[2,256,256]{2,1,0:T(8,128)} %h_static.1) | copy-start | bytes 1572868
  3.2 1.0 %copy-start.3 = (f32[2,256,256]{2,1,0:T(8,128)S(1)}, f32[2,256,256]{2,1,0:T(8,128)}, u32[]{:S(2)}) copy-start(f32[2,256,256]{2,1,0:T(8,128)} %drive_op.1) | copy-start | bytes 1572868
  4.3 0.7 copy-start.4
  4.9 0.7 copy-start.5
  5.6 0.7 copy-start.6
  6.3 0.7 copy-start.7
  6.9 0.7 copy-start.8
where the time goes:
time: 96.1 us; the launch traced here: 95.8 us
  Pallas kernels  87.4 us (91%)
  local copies, waits for them, and re-layouts  8.35 us (9%)
    pallas_call x1, Pallas kernels, on_device(): pl.pallas_call(functools.partial(kernel, count), out_shape=jax.ShapeDtype...  87.4 us
    unnamed x19, local copies, waits for them, and re-layouts  8.35 us

commit v1 on v0

v1 whole, which is shorter than its diff:
```python
import functools

import jax
import jax.numpy as jnp
import numpy as np
from jax import lax
from jax.experimental import pallas as pl
from jax.experimental.pallas import tpu as pltpu
from jax.sharding import PartitionSpec as P

MESH = pl.DeviceIdType.MESH
STEP = 0.05
AMP = 2.0
FREQ = 20.0
M = 256
HALF = 128
MODES = 3
STAGES = 4
SIB, FAR, NEAR, BACK, OWN = range(5)
RE, IM = 0, 1
BF = jnp.bfloat16
F32 = jnp.float32


def split(value):
    high = value.astype(BF)
    return high, (value - high.astype(F32)).astype(BF)


def kernel(
    count,
    bath_hbm,
    damp_hbm,
    occ_hbm,
    up_hbm,
    down_hbm,
    state,
    h_static,
    drive_op,
    couple,
    out,
    bath,
    damp,
    occ,
    up,
    down,
    ybuf,
    win,
    raw,
    herm,
    left_of,
    right_of,
    total,
    acc,
    load_sem,
    send_sem,
    recv_sem,
):
    me = lax.axis_index("aux")
    odd = lax.rem(me, 2)
    even = odd == 0
    d = 1 - 2 * odd

    def at(offset):
        return lax.rem(me + offset + count, count)

    partner = [at(d), at(2 * d), at(-d), at(-2 * d)]
    chip = me // 2
    last = count // 2 - 1
    has_far = (chip + d >= 0) & (chip + d <= last)
    has_back = (chip - d >= 0) & (chip - d <= last)

    moves = [
        (state.at[0], ybuf.at[0]),
        (h_static, raw.at[pl.ds(3, 2)]),
        (drive_op, raw.at[pl.ds(5, 2)]),
        (couple, raw.at[pl.ds(0, 3)]),
        (bath_hbm, bath),
        (damp_hbm, damp),
        (occ_hbm, occ),
        (up_hbm, up),
        (down_hbm, down),
    ]
    loads = [
        pltpu.make_async_copy(src, dst, load_sem.at[i])
        for i, (src, dst) in enumerate(moves)
    ]
    for load in loads:
        load.start()

    barrier = pltpu.get_barrier_semaphore()

    def greet(slot):
        pl.semaphore_signal(
            barrier, inc=1, device_id=(partner[slot],), device_id_type=MESH
        )

    greet(SIB)

    @pl.when(has_far)
    def _():
        greet(FAR)

    @pl.when(has_back)
    def _():
        greet(NEAR)
        greet(BACK)

    pl.semaphore_wait(
        barrier, 1 + jnp.where(has_far, 1, 0) + jnp.where(has_back, 2, 0)
    )

    def rows(ref, half):
        return ref if half is None else ref.at[pl.ds(half * HALF, HALF)]

    def remote(src, stage, slot, plane, half, number, device):
        part = 0 if half is None else half
        return pltpu.make_async_remote_copy(
            src_ref=rows(src, half),
            dst_ref=rows(win.at[stage, slot, plane], half),
            send_sem=send_sem.at[stage, number, part],
            recv_sem=recv_sem.at[stage, slot, plane, part],
            device_id=(device,),
            device_id_type=MESH,
        )

    def to_back_real(stage):
        return [remote(ybuf.at[stage, RE], stage, FAR, RE, None, 0, partner[BACK])]

    def to_back_imag(stage):
        return [remote(ybuf.at[stage, IM], stage, NEAR, IM, 0, 1, partner[NEAR])]

    def to_back_late(stage):
        return [remote(win.at[stage, SIB, IM], stage, BACK, IM, 1, 1, partner[NEAR])]

    def to_far_real(stage):
        return [remote(ybuf.at[stage, RE], stage, BACK, RE, 0, 2, partner[FAR])]

    def to_far_late(stage):
        return [
            remote(win.at[stage, SIB, IM], stage, NEAR, IM, 1, 3, partner[FAR]),
            remote(ybuf.at[stage, RE], stage, BACK, RE, 1, 2, partner[FAR]),
            remote(ybuf.at[stage, IM], stage, BACK, IM, 0, 3, partner[FAR]),
        ]

    def to_sibling(stage):
        return [
            remote(ybuf.at[stage, IM], stage, SIB, IM, 1, 4, partner[SIB]),
            remote(ybuf.at[stage, IM], stage, SIB, IM, 0, 4, partner[SIB]),
            remote(ybuf.at[stage, RE], stage, SIB, RE, None, 5, partner[SIB]),
        ]

    def hand_real(stage):
        return [remote(win.at[stage, FAR, RE], stage, NEAR, RE, None, 6, partner[SIB])]

    def hand_imag(stage, half):
        return [remote(win.at[stage, NEAR, IM], stage, FAR, IM, half, 7, partner[SIB])]

    def start(copies):
        for copy in copies:
            copy.start()

    def send_real(stage):
        @pl.when(has_back)
        def _():
            start(to_back_real(stage))

        @pl.when(has_far)
        def _():
            start(to_far_real(stage))

    def send_imag(stage):
        @pl.when(has_back)
        def _():
            start(to_back_imag(stage))

        start(to_sibling(stage))

    def arrived(stage, slot, plane, half=None):
        remote(
            win.at[stage, slot, plane], stage, slot, plane, half, 0, partner[SIB]
        ).wait_recv()

    def send_late(stage):
        arrived(stage, SIB, IM, 1)

        @pl.when(has_far)
        def _():
            start(to_far_late(stage))

        @pl.when(has_back)
        def _():
            start(to_back_late(stage))

    loads[0].wait()
    send_real(0)
    send_imag(0)

    def put(slot, real, imag, imag_right):
        for row, value in ((0, real), (M, imag)):
            high, low = split(value)
            left_of[slot, pl.ds(row, M), pl.ds(0, M)] = high
            left_of[slot, pl.ds(row, M), pl.ds(M, M)] = low
            left_of[slot, pl.ds(row, M), pl.ds(2 * M, M)] = high
        for column, value in ((0, real), (M, imag_right)):
            high, low = split(value)
            right_of[slot, pl.ds(0, M), pl.ds(column, M)] = high
            right_of[slot, pl.ds(M, M), pl.ds(column, M)] = low
            right_of[slot, pl.ds(2 * M, M), pl.ds(column, M)] = high

    def products(slot, value, wide, begin=0):
        high, low = split(value)
        size = 2 * M if wide else M
        left = jnp.dot(
            left_of[slot, pl.ds(begin, size)],
            jnp.concatenate([high, high, low], axis=0),
            preferred_element_type=F32,
        )
        right = jnp.dot(
            jnp.concatenate([high, high, low], axis=1),
            right_of[slot, :, pl.ds(begin, size)],
            preferred_element_type=F32,
        )
        return left, right

    def own_products(stage):
        slot = OWN + (stage + 1) // 2
        real, imag = ybuf[stage, RE], ybuf[stage, IM]
        left, right = products(slot, real, True)
        total[0] = rate * imag + (left[:M] - right[:, :M])
        total[1] = (left[M:] + right[:, M:]) - rate * real
        left, right = products(slot, imag, True)
        total[0] -= left[M:] + right[:, M:]
        total[1] += left[:M] - right[:, :M]

    def take_complex(stage, slot, plane):
        left, right = products(slot, win[stage, slot, plane], True)
        minus = left[:M] - right[:, :M]
        plus = left[M:] + right[:, M:]
        if plane == RE:
            total[0] += minus
            total[1] += plus
        else:
            total[0] -= plus
            total[1] += minus

    def take_real(stage, slot, plane):
        left, right = products(slot, win[stage, slot, plane], False)
        total[plane] += left - right

    def take(stage, slot, plane):
        real = even if slot in (SIB, FAR) else jnp.logical_not(even)

        @pl.when(real)
        def _():
            take_real(stage, slot, plane)

        @pl.when(jnp.logical_not(real))
        def _():
            take_complex(stage, slot, plane)

    drive = [
        np.float32(AMP) * np.cos(np.float32(FREQ * t)) for t in (0.0, STEP / 2, STEP)
    ]

    def put_own(i):
        real = herm[0, 0] + drive[i] * herm[1, 0]
        imag = herm[0, 1] + drive[i] * herm[1, 1]
        put(OWN + i, real, imag, -imag)

    for load in loads[4:]:
        load.wait()
    rate = jnp.float32(0.0)
    for k in range(MODES):
        rate = rate + occ[0, k].astype(F32) * damp[k]

    loads[1].wait()
    loads[2].wait()
    for k in range(2):
        value = raw[3 + 2 * k]
        herm[k, 0] = (value + value.T) * 0.5
        value = raw[4 + 2 * k]
        herm[k, 1] = (value - value.T) * 0.5
    put_own(0)
    own_products(0)
    send_late(0)

    loads[3].wait()
    for k in range(MODES):
        value = raw[k]
        raw[k] = (value + value.T) * 0.5

    for slot in range(4):
        real = jnp.zeros((M, M), F32)
        imag = jnp.zeros((M, M), F32)
        for k in range(MODES):
            raises = jnp.where(up[0, k] == partner[slot], 1.0, 0.0).astype(F32)
            lowers = jnp.where(
                down[0, k] == partner[slot], occ[0, k].astype(F32), 0.0
            ).astype(F32)
            real = real + (raises + lowers * bath[0, k]) * raw[k]
            imag = imag + (lowers * bath[1, k]) * raw[k]
        put(slot, real, imag, imag)

    put_own(1)
    put_own(2)
    acc[...] = jnp.zeros_like(acc)

    def stage_body(stage, carry):
        arrived(stage, SIB, IM, 0)
        arrived(stage, SIB, RE)
        take(stage, SIB, RE)
        take(stage, SIB, IM)

        @pl.when(has_far)
        def _():
            arrived(stage, FAR, RE)
            start(hand_real(stage))

        @pl.when(has_back)
        def _():
            arrived(stage, NEAR, IM, 1)
            start(hand_imag(stage, 1))

        @pl.when(has_far)
        def _():
            take(stage, FAR, RE)

        @pl.when(has_back)
        def _():
            arrived(stage, NEAR, IM, 0)
            start(hand_imag(stage, 0))
            arrived(stage, NEAR, RE)
            take(stage, NEAR, RE)
            take(stage, NEAR, IM)
            arrived(stage, BACK, RE, 0)
            arrived(stage, BACK, RE, 1)
            take(stage, BACK, RE)

        @pl.when(has_far)
        def _():
            arrived(stage, FAR, IM, 1)
            arrived(stage, FAR, IM, 0)
            take(stage, FAR, IM)

        @pl.when(has_back)
        def _():
            arrived(stage, BACK, IM, 0)
            arrived(stage, BACK, IM, 1)
            take_real(stage, BACK, IM)

        ahead = jnp.where(stage == 2, STEP, STEP / 2).astype(F32)

        @pl.when(stage < STAGES - 1)
        def _():
            ybuf[stage + 1, RE] = ybuf[0, RE] + ahead * total[1]
            send_real(stage + 1)

        @pl.when(has_back & even)
        def _():
            left, right = products(BACK, win[stage, BACK, IM], False, M)
            total[0] -= left + right

        @pl.when(stage < STAGES - 1)
        def _():
            ybuf[stage + 1, IM] = ybuf[0, IM] - ahead * total[0]
            send_imag(stage + 1)
            weight = jnp.where(stage == 0, 1.0, 2.0).astype(F32)
            acc[RE] += weight * total[1]
            acc[IM] -= weight * total[0]
            own_products(stage + 1)
            send_late(stage + 1)

        return carry

    lax.fori_loop(0, STAGES, stage_body, 0)

    out[0, RE] = ybuf[0, RE] + (STEP / 6) * (acc[RE] + total[1])
    out[0, IM] = ybuf[0, IM] + (STEP / 6) * (acc[IM] - total[0])

    def drain(stage, carry):
        for copy in to_sibling(stage):
            copy.wait_send()

        @pl.when(has_back)
        def _():
            for copy in [
                *to_back_real(stage),
                *to_back_imag(stage),
                *to_back_late(stage),
                *hand_imag(stage, 0),
                *hand_imag(stage, 1),
            ]:
                copy.wait_send()

        @pl.when(has_far)
        def _():
            for copy in [
                *to_far_real(stage),
                *to_far_late(stage),
                *hand_real(stage),
            ]:
                copy.wait_send()

        return carry

    lax.fori_loop(0, STAGES, drain, 0)


def on_device(
    state, h_static, drive_op, couple, bath_coef, damping, occupation, raise_nbr, lower_nbr
):
    count = lax.axis_size("aux")
    return pl.pallas_call(
        functools.partial(kernel, count),
        out_shape=jax.ShapeDtypeStruct(state.shape, F32),
        in_specs=[pl.BlockSpec(memory_space=pltpu.HBM)] * 9,
        out_specs=pl.BlockSpec(memory_space=pltpu.VMEM),
        scratch_shapes=[
            pltpu.SMEM((2, MODES), F32),
            pltpu.SMEM((MODES,), F32),
            pltpu.SMEM((1, MODES), jnp.int32),
            pltpu.SMEM((1, MODES), jnp.int32),
            pltpu.SMEM((1, MODES), jnp.int32),
            pltpu.VMEM((STAGES, 2, M, M), F32),
            pltpu.VMEM((STAGES, 4, 2, M, M), F32),
            pltpu.VMEM((7, M, M), F32),
            pltpu.VMEM((2, 2, M, M), F32),
            pltpu.VMEM((OWN + 3, 2 * M, 3 * M), BF),
            pltpu.VMEM((OWN + 3, 3 * M, 2 * M), BF),
            pltpu.VMEM((2, M, M), F32),
            pltpu.VMEM((2, M, M), F32),
            pltpu.SemaphoreType.DMA((9,)),
            pltpu.SemaphoreType.DMA((STAGES, 8, 2)),
            pltpu.SemaphoreType.DMA((STAGES, 4, 2, 2)),
        ],
        compiler_params=pltpu.CompilerParams(
            collective_id=0, has_side_effects=True, vmem_limit_bytes=48 << 20
        ),
        name="rk_step",
    )(
        *(
            pltpu.with_memory_space_constraint(x, pltpu.HBM)
            for x in (
                bath_coef,
                damping,
                occupation,
                raise_nbr,
                lower_nbr,
                state,
                h_static,
                drive_op,
                couple,
            )
        )
    )


def solution(mesh):
    return jax.shard_map(
        on_device,
        mesh=mesh,
        in_specs=(
            P("aux", None, None, None),
            P(),
            P(),
            P(),
            P(),
            P(),
            P("aux", None),
            P("aux", None),
            P("aux", None),
        ),
        out_specs=P("aux", None, None, None),
        check_vma=False,
    )
```

time: 96.1 us -> 69.5 us (0.72)
  the two profiles are of different devices: /device:TPU:1 before, /device:TPU:24 now
where the time goes in v1:
time: 69.5 us; the launch traced here: 69.4 us
  Pallas kernels  68.5 us (99%)
  local copies, waits for them, and re-layouts  0.8 us (1%)
    pallas_call x1, Pallas kernels, on_device(): pl.pallas_call(functools.partial(kernel, count), out_shape=jax.ShapeDtype...  68.5 us

profile of v1, /device:TPU:24, one launch (start us, length us, event | category | flops | bytes accessed | tf_op | source)
XLA Modules:
  0.0 69.4 jit_solution(11433112448349664621)
XLA Ops:
  0.0 68.5 %rk_step.1 = f32[1,2,256,256]{3,2,1,0:T(8,128)S(1)} custom-call(f32[2,3]{1,0:T(2,128)} %bath_hbm.1, f32[3]{0:T(128)} %damp_hbm.1, s32[1,3]{1,0:T(1,128)} %occ_hbm.1, s32[1,3]{1,0:T(1,128)} %up_hbm.1, s32[1,3]{1,0:T(1,128)} %down_hbm.1, f32[1,2,256,256]{3,2,1,0:T(8,128)} %state.1, f32[2,256,256]{2,1,0:T(8,128)} %h_static.1, f32[2,256,256]{2,1,0:T(8,128)} %drive_op.1, ...), custom_call_target="tpu_custom_call" | custom-call | tf_op jit(solution)/shard_map/rk_step/pallas_call | solution.py:414
  68.6 0.8 %copy.11 = f32[1,2,256,256]{3,2,1,0:T(8,128)} copy(f32[1,2,256,256]{3,2,1,0:T(8,128)S(1)} %rk_step.1) | data formatting | bytes 1048576

commit v2 on v1

--- a/solution.py
+++ b/solution.py
@@ -14,6 +14,7 @@
 FREQ = 20.0
 M = 256
 HALF = 128
+ROW = 16
 MODES = 3
 STAGES = 4
 SIB, FAR, NEAR, BACK, OWN = range(5)
@@ -52,9 +53,19 @@
     right_of,
     total,
     acc,
+    rim,
+    zbuf,
+    zsib,
+    rim_left,
+    rim_right,
+    extra,
     load_sem,
     send_sem,
     recv_sem,
+    rim_send,
+    rim_recv,
+    z_send,
+    z_recv,
 ):
     me = lax.axis_index("aux")
     odd = lax.rem(me, 2)
@@ -69,6 +80,10 @@
     last = count // 2 - 1
     has_far = (chip + d >= 0) & (chip + d <= last)
     has_back = (chip - d >= 0) & (chip - d <= last)
+
+    below = (lax.rem(chip, ROW) == ROW - 1) & (chip < last)
+    above = (lax.rem(chip, ROW) == 0) & (chip > 0)
+    odd_one = jnp.logical_not(even)
 
     moves = [
         (state.at[0], ybuf.at[0]),
@@ -124,24 +139,34 @@
             device_id_type=MESH,
         )
 
-    def to_back_real(stage):
-        return [remote(ybuf.at[stage, RE], stage, FAR, RE, None, 0, partner[BACK])]
-
-    def to_back_imag(stage):
-        return [remote(ybuf.at[stage, IM], stage, NEAR, IM, 0, 1, partner[NEAR])]
-
-    def to_back_late(stage):
-        return [remote(win.at[stage, SIB, IM], stage, BACK, IM, 1, 1, partner[NEAR])]
-
-    def to_far_real(stage):
-        return [remote(ybuf.at[stage, RE], stage, BACK, RE, 0, 2, partner[FAR])]
-
-    def to_far_late(stage):
+    def to_back_real(stage, own):
+        return [remote(own.at[RE], stage, FAR, RE, None, 0, partner[BACK])]
+
+    def to_back_imag(stage, own):
+        return [remote(own.at[IM], stage, NEAR, IM, 0, 1, partner[NEAR])]
+
+    def to_back_late(stage, other):
+        return [halfway(other, stage, BACK, 1, partner[NEAR])]
+
+    def to_far_real(stage, own):
+        return [remote(own.at[RE], stage, BACK, RE, 0, 2, partner[FAR])]
+
+    def to_far_late(stage, own, other):
         return [
-            remote(win.at[stage, SIB, IM], stage, NEAR, IM, 1, 3, partner[FAR]),
-            remote(ybuf.at[stage, RE], stage, BACK, RE, 1, 2, partner[FAR]),
-            remote(ybuf.at[stage, IM], stage, BACK, IM, 0, 3, partner[FAR]),
+            halfway(other, stage, NEAR, 3, partner[FAR]),
+            remote(own.at[RE], stage, BACK, RE, 1, 2, partner[FAR]),
+            remote(own.at[IM], stage, BACK, IM, 0, 3, partner[FAR]),
         ]
+
+    def halfway(other, stage, slot, number, device):
+        return pltpu.make_async_remote_copy(
+            src_ref=other,
+            dst_ref=rows(win.at[stage, slot, IM], 1),
+            send_sem=send_sem.at[stage, number, 1],
+            recv_sem=recv_sem.at[stage, slot, IM, 1],
+            device_id=(device,),
+            device_id_type=MESH,
+        )
 
     def to_sibling(stage):
         return [
@@ -150,6 +175,26 @@
             remote(ybuf.at[stage, RE], stage, SIB, RE, None, 5, partner[SIB]),
         ]
 
+    def part_to_sibling(stage):
+        return pltpu.make_async_remote_copy(
+            src_ref=rows(zbuf.at[stage, IM], 1),
+            dst_ref=zsib.at[stage],
+            send_sem=z_send.at[stage],
+            recv_sem=z_recv.at[stage],
+            device_id=(partner[SIB],),
+            device_id_type=MESH,
+        )
+
+    def rim_row(i, slot):
+        return pltpu.make_async_remote_copy(
+            src_ref=up_hbm,
+            dst_ref=rim.at[i],
+            send_sem=rim_send.at[0 if slot != BACK else 1],
+            recv_sem=rim_recv.at[i],
+            device_id=(partner[slot],),
+            device_id_type=MESH,
+        )
+
     def hand_real(stage):
         return [remote(win.at[stage, FAR, RE], stage, NEAR, RE, None, 6, partner[SIB])]
 
@@ -160,41 +205,56 @@
         for copy in copies:
             copy.start()
 
-    def send_real(stage):
+    def back_real(stage, own):
         @pl.when(has_back)
         def _():
-            start(to_back_real(stage))
-
+            start(to_back_real(stage, own))
+
+    def far_real(stage, own):
         @pl.when(has_far)
         def _():
-            start(to_far_real(stage))
-
-    def send_imag(stage):
+            start(to_far_real(stage, own))
+
+    def back_imag(stage, own):
         @pl.when(has_back)
         def _():
-            start(to_back_imag(stage))
-
-        start(to_sibling(stage))
+            start(to_back_imag(stage, own))
 
     def arrived(stage, slot, plane, half=None):
         remote(
             win.at[stage, slot, plane], stage, slot, plane, half, 0, partner[SIB]
         ).wait_recv()
 
+    def late_far(stage, own, other):
+        @pl.when(has_far)
+        def _():
+            start(to_far_late(stage, own, other))
+
+    def late_back(stage, other):
+        @pl.when(has_back)
+        def _():
+            start(to_back_late(stage, other))
+
     def send_late(stage):
         arrived(stage, SIB, IM, 1)
-
-        @pl.when(has_far)
-        def _():
-            start(to_far_late(stage))
-
-        @pl.when(has_back)
-        def _():
-            start(to_back_late(stage))
+        other = rows(win.at[stage, SIB, IM], 1)
+        late_far(stage, ybuf.at[stage], other)
+        late_back(stage, other)
 
     loads[0].wait()
-    send_real(0)
-    send_imag(0)
+    back_real(0, ybuf.at[0])
+    far_real(0, ybuf.at[0])
+    back_imag(0, ybuf.at[0])
+    start(to_sibling(0))
+
+    @pl.when(below & even)
+    def _():
+        rim_row(1, FAR).start()
+
+    @pl.when(below & odd_one)
+    def _():
+        rim_row(0, NEAR).start()
+        rim_row(0, BACK).start()
 
     def put(slot, real, imag, imag_right):
         for row, value in ((0, real), (M, imag)):
@@ -233,8 +293,19 @@
         total[0] -= left[M:] + right[:, M:]
         total[1] += left[:M] - right[:, :M]
 
+    def received(stage, slot, plane):
+        value = win[stage, slot, plane]
+        if slot == SIB:
+            return value
+        who = odd_one if slot == FAR else even
+        before = jnp.where(stage == STAGES - 1, STEP, STEP / 2).astype(F32)
+        scale = jnp.where(above & who & (stage > 0), before, 0.0).astype(F32)
+        which = 1 if slot == BACK else 0
+        other = extra[lax.rem(stage, 2), which, 1 - plane]
+        return value + (scale if plane == RE else -scale) * other
+
     def take_complex(stage, slot, plane):
-        left, right = products(slot, win[stage, slot, plane], True)
+        left, right = products(slot, received(stage, slot, plane), True)
         minus = left[:M] - right[:, :M]
         plus = left[M:] + right[:, M:]
         if plane == RE:
@@ -245,8 +316,35 @@
             total[1] += minus
 
     def take_real(stage, slot, plane):
-        left, right = products(slot, win[stage, slot, plane], False)
+        left, right = products(slot, received(stage, slot, plane), False)
         total[plane] += left - right
+
+    def contribution(i, value):
+        high, low = split(value)
+        left = jnp.dot(
+            rim_left[i],
+            jnp.concatenate([high, high, low], axis=0),
+            preferred_element_type=F32,
+        )
+        right = jnp.dot(
+            jnp.concatenate([high, high, low], axis=1),
+            rim_right[i],
+            preferred_element_type=F32,
+        )
+        return left - right
+
+    def contribute(stage):
+        later = lax.rem(stage + 1, 2)
+        for plane in (RE, IM):
+            own = ybuf[stage, plane]
+            extra[later, 0, plane] = contribution(0, own) + contribution(
+                1, win[stage, SIB, plane]
+            )
+
+        @pl.when(even)
+        def _():
+            for plane in (RE, IM):
+                extra[later, 1, plane] = contribution(2, ybuf[stage, plane])
 
     def take(stage, slot, plane):
         real = even if slot in (SIB, FAR) else jnp.logical_not(even)
@@ -305,13 +403,29 @@
     put_own(1)
     put_own(2)
     acc[...] = jnp.zeros_like(acc)
-
-    def stage_body(stage, carry):
-        arrived(stage, SIB, IM, 0)
-        arrived(stage, SIB, RE)
-        take(stage, SIB, RE)
-        take(stage, SIB, IM)
-
+    extra[...] = jnp.zeros_like(extra)
+
+    def put_rim(i, row, source):
+        real = jnp.zeros((M, M), F32)
+        for k in range(MODES):
+            real = real + jnp.where(rim[row, 0, k] == source, 1.0, 0.0).astype(F32) * raw[k]
+        high, low = split(real)
+        for j, part in enumerate((high, low, high)):
+            rim_left[i, :, pl.ds(j * M, M)] = part
+            rim_right[i, pl.ds(j * M, M), :] = part
+
+    @pl.when(above)
+    def _():
+        rim_row(0, NEAR).wait_recv()
+        put_rim(0, 0, me)
+        put_rim(1, 0, partner[SIB])
+
+    @pl.when(above & even)
+    def _():
+        rim_row(1, NEAR).wait_recv()
+        put_rim(2, 1, me)
+
+    def usual(stage, ahead):
         @pl.when(has_far)
         def _():
             arrived(stage, FAR, RE)
@@ -349,27 +463,157 @@
             arrived(stage, BACK, IM, 1)
             take_real(stage, BACK, IM)
 
+        after = stage + 1
+
+        @pl.when(stage < STAGES - 1)
+        def _():
+            ybuf[after, RE] = ybuf[0, RE] + ahead * total[1]
+            back_real(after, ybuf.at[after])
+            far_real(after, ybuf.at[after])
+
+        @pl.when(has_back & even)
+        def _():
+            value = received(stage, BACK, IM)
+            left, right = products(BACK, value, False, M)
+            total[0] -= left + right
+
+        @pl.when(stage < STAGES - 1)
+        def _():
+            ybuf[after, IM] = ybuf[0, IM] - ahead * total[0]
+            back_imag(after, ybuf.at[after])
+            start(to_sibling(after))
+
+    def keep_part(after, ahead):
+        zbuf[after, RE] = ybuf[0, RE] + ahead * total[1]
+        zbuf[after, IM] = ybuf[0, IM] - ahead * total[0]
+
+    def below_even(stage, ahead):
+        after = stage + 1
+        arrived(stage, NEAR, IM, 1)
+        start(hand_imag(stage, 1))
+        arrived(stage, FAR, RE)
+        start(hand_real(stage))
+        arrived(stage, NEAR, IM, 0)
+        start(hand_imag(stage, 0))
+        arrived(stage, NEAR, RE)
+        take_complex(stage, NEAR, RE)
+        take_complex(stage, NEAR, IM)
+        arrived(stage, BACK, RE, 0)
+        arrived(stage, BACK, RE, 1)
+        take_complex(stage, BACK, RE)
+        arrived(stage, BACK, IM, 0)
+        arrived(stage, BACK, IM, 1)
+        take_complex(stage, BACK, IM)
+
+        @pl.when(stage < STAGES - 1)
+        def _():
+            keep_part(after, ahead)
+            start(to_far_real(after, zbuf.at[after]))
+            part_to_sibling(after).start()
+
+        take_real(stage, FAR, RE)
+        arrived(stage, FAR, IM, 1)
+        arrived(stage, FAR, IM, 0)
+        take_real(stage, FAR, IM)
+
+        @pl.when(stage < STAGES - 1)
+        def _():
+            ybuf[after, RE] = ybuf[0, RE] + ahead * total[1]
+            start(to_back_real(after, ybuf.at[after]))
+            ybuf[after, IM] = ybuf[0, IM] - ahead * total[0]
+            start(to_back_imag(after, ybuf.at[after]))
+            start(to_sibling(after))
+
+    def below_odd(stage, ahead):
+        after = stage + 1
+        arrived(stage, FAR, RE)
+        start(hand_real(stage))
+        take_complex(stage, FAR, RE)
+        arrived(stage, NEAR, IM, 1)
+        start(hand_imag(stage, 1))
+        arrived(stage, NEAR, IM, 0)
+        start(hand_imag(stage, 0))
+        arrived(stage, FAR, IM, 1)
+        arrived(stage, FAR, IM, 0)
+        take_complex(stage, FAR, IM)
+
+        @pl.when(stage < STAGES - 1)
+        def _():
+            keep_part(after, ahead)
+            start(to_back_real(after, zbuf.at[after]))
+            start(to_back_imag(after, zbuf.at[after]))
+            part_to_sibling(after).start()
+
+        take_real(stage, NEAR, IM)
+        arrived(stage, NEAR, RE)
+        take_real(stage, NEAR, RE)
+        arrived(stage, BACK, RE, 0)
+        arrived(stage, BACK, RE, 1)
+        take_real(stage, BACK, RE)
+        arrived(stage, BACK, IM, 0)
+        arrived(stage, BACK, IM, 1)
+        take_real(stage, BACK, IM)
+
+        @pl.when(stage < STAGES - 1)
+        def _():
+            ybuf[after, RE] = ybuf[0, RE] + ahead * total[1]
+            start(to_far_real(after, ybuf.at[after]))
+            ybuf[after, IM] = ybuf[0, IM] - ahead * total[0]
+            start(to_sibling(after))
+
+    def late_below(stage):
+        arrived(stage, SIB, IM, 1)
+        part_to_sibling(stage).wait_recv()
+        other = rows(win.at[stage, SIB, IM], 1)
+
+        @pl.when(even)
+        def _():
+            start(to_far_late(stage, zbuf.at[stage], zsib.at[stage]))
+            start(to_back_late(stage, other))
+
+        @pl.when(odd_one)
+        def _():
+            start(to_far_late(stage, ybuf.at[stage], other))
+            start(to_back_late(stage, zsib.at[stage]))
+
+    def stage_body(stage, carry):
+        arrived(stage, SIB, IM, 0)
+        arrived(stage, SIB, RE)
+        take(stage, SIB, RE)
+        take(stage, SIB, IM)
+
+        @pl.when(above & (stage < STAGES - 1))
+        def _():
+            contribute(stage)
+
         ahead = jnp.where(stage == 2, STEP, STEP / 2).astype(F32)
 
+        @pl.when(jnp.logical_not(below))
+        def _():
+            usual(stage, ahead)
+
+        @pl.when(below & even)
+        def _():
+            below_even(stage, ahead)
+
+        @pl.when(below & odd_one)
+        def _():
+            below_odd(stage, ahead)
+
         @pl.when(stage < STAGES - 1)
         def _():
-            ybuf[stage + 1, RE] = ybuf[0, RE] + ahead * total[1]
-            send_real(stage + 1)
-
-        @pl.when(has_back & even)
-        def _():
-            left, right = products(BACK, win[stage, BACK, IM], False, M)
-            total[0] -= left + right
-
-        @pl.when(stage < STAGES - 1)
-        def _():
-            ybuf[stage + 1, IM] = ybuf[0, IM] - ahead * total[0]
-            send_imag(stage + 1)
             weight = jnp.where(stage == 0, 1.0, 2.0).astype(F32)
             acc[RE] += weight * total[1]
             acc[IM] -= weight * total[0]
             own_products(stage + 1)
+
+        @pl.when((stage < STAGES - 1) & jnp.logical_not(below))
+        def _():
             send_late(stage + 1)
+
+        @pl.when((stage < STAGES - 1) & below)
+        def _():
+            late_below(stage + 1)
 
         return carry
 
@@ -385,9 +629,9 @@
         @pl.when(has_back)
         def _():
             for copy in [
-                *to_back_real(stage),
-                *to_back_imag(stage),
-                *to_back_late(stage),
+                *to_back_real(stage, ybuf.at[stage]),
+                *to_back_imag(stage, ybuf.at[stage]),
+                *to_back_late(stage, zsib.at[stage]),
                 *hand_imag(stage, 0),
                 *hand_imag(stage, 1),
             ]:
@@ -396,15 +640,28 @@
         @pl.when(has_far)
         def _():
             for copy in [
-                *to_far_real(stage),
-                *to_far_late(stage),
+                *to_far_real(stage, ybuf.at[stage]),
+                *to_far_late(stage, ybuf.at[stage], zsib.at[stage]),
                 *hand_real(stage),
             ]:
                 copy.wait_send()
 
+        @pl.when(below & (stage > 0))
+        def _():
+            part_to_sibling(stage).wait_send()
+
         return carry
 
     lax.fori_loop(0, STAGES, drain, 0)
+
+    @pl.when(below & even)
+    def _():
+        rim_row(1, FAR).wait_send()
+
+    @pl.when(below & odd_one)
+    def _():
+        rim_row(0, NEAR).wait_send()
+        rim_row(0, BACK).wait_send()
 
 
 def on_device(
@@ -430,9 +687,19 @@
             pltpu.VMEM((OWN + 3, 3 * M, 2 * M), BF),
             pltpu.VMEM((2, M, M), F32),
             pltpu.VMEM((2, M, M), F32),
+            pltpu.SMEM((2, 1, MODES), jnp.int32),
+            pltpu.VMEM((STAGES, 2, M, M), F32),
+            pltpu.VMEM((STAGES, HALF, M), F32),
+            pltpu.VMEM((3, M, 3 * M), BF),
+            pltpu.VMEM((3, 3 * M, M), BF),
+            pltpu.VMEM((2, 2, 2, M, M), F32),
             pltpu.SemaphoreType.DMA((9,)),
             pltpu.SemaphoreType.DMA((STAGES, 8, 2)),
             pltpu.SemaphoreType.DMA((STAGES, 4, 2, 2)),
+            pltpu.SemaphoreType.DMA((2,)),
+            pltpu.SemaphoreType.DMA((2,)),
+            pltpu.SemaphoreType.DMA((STAGES,)),
+            pltpu.SemaphoreType.DMA((STAGES,)),
         ],
         compiler_params=pltpu.CompilerParams(
             collective_id=0, has_side_effects=True, vmem_limit_bytes=48 << 20

time: 69.5 us -> 66.6 us (0.958)
  Pallas kernels: 68.5 us -> 65.7 us
    pallas_call x1, Pallas kernels: 68.5 us -> 65.7 us  [on_device(): pl.pallas_call(functools.partial(kernel, count), out_shape=jax.ShapeDtype...]
where the time goes in v2:
time: 66.6 us; the launch traced here: 66.5 us
  Pallas kernels  65.7 us (99%)
  local copies, waits for them, and re-layouts  0.8 us (1%)
    pallas_call x1, Pallas kernels, on_device(): pl.pallas_call(functools.partial(kernel, count), out_shape=jax.ShapeDtype...  65.7 us

profile of v2, /device:TPU:24, one launch (start us, length us, event | category | flops | bytes accessed | tf_op | source)
XLA Modules:
  0.0 66.5 jit_solution(5937442249048001327)
XLA Ops:
  0.0 65.7 %rk_step.1 = f32[1,2,256,256]{3,2,1,0:T(8,128)S(1)} custom-call(f32[2,3]{1,0:T(2,128)} %bath_hbm.1, f32[3]{0:T(128)} %damp_hbm.1, s32[1,3]{1,0:T(1,128)} %occ_hbm.1, s32[1,3]{1,0:T(1,128)} %up_hbm.1, s32[1,3]{1,0:T(1,128)} %down_hbm.1, f32[1,2,256,256]{3,2,1,0:T(8,128)} %state.1, f32[2,256,256]{2,1,0:T(8,128)} %h_static.1, f32[2,256,256]{2,1,0:T(8,128)} %drive_op.1, ...), custom_call_target="tpu_custom_call" | custom-call | tf_op jit(solution)/shard_map/rk_step/pallas_call | solution.py:671
  65.7 0.8 %copy.11 = f32[1,2,256,256]{3,2,1,0:T(8,128)} copy(f32[1,2,256,256]{3,2,1,0:T(8,128)S(1)} %rk_step.1) | data formatting | bytes 1048576

commit v3 on v2

--- a/solution.py
+++ b/solution.py
@@ -18,6 +18,7 @@
 MODES = 3
 STAGES = 4
 SIB, FAR, NEAR, BACK, OWN = range(5)
+TO_SIB, TO_BACK, TO_FAR = range(3)
 RE, IM = 0, 1
 BF = jnp.bfloat16
 F32 = jnp.float32
@@ -96,6 +97,24 @@
         (up_hbm, up),
         (down_hbm, down),
     ]
+    barrier = pltpu.get_barrier_semaphore()
+
+    def greet(slot):
+        pl.semaphore_signal(
+            barrier, inc=1, device_id=(partner[slot],), device_id_type=MESH
+        )
+
+    greet(SIB)
+
+    @pl.when(has_far)
+    def _():
+        greet(FAR)
+
+    @pl.when(has_back)
+    def _():
+        greet(NEAR)
+        greet(BACK)
+
     loads = [
         pltpu.make_async_copy(src, dst, load_sem.at[i])
         for i, (src, dst) in enumerate(moves)
@@ -103,24 +122,6 @@
     for load in loads:
         load.start()
 
-    barrier = pltpu.get_barrier_semaphore()
-
-    def greet(slot):
-        pl.semaphore_signal(
-            barrier, inc=1, device_id=(partner[slot],), device_id_type=MESH
-        )
-
-    greet(SIB)
-
-    @pl.when(has_far)
-    def _():
-        greet(FAR)
-
-    @pl.when(has_back)
-    def _():
-        greet(NEAR)
-        greet(BACK)
-
     pl.semaphore_wait(
         barrier, 1 + jnp.where(has_far, 1, 0) + jnp.where(has_back, 2, 0)
     )
@@ -128,59 +129,71 @@
     def rows(ref, half):
         return ref if half is None else ref.at[pl.ds(half * HALF, HALF)]
 
-    def remote(src, stage, slot, plane, half, number, device):
-        part = 0 if half is None else half
+    def flag(stage, slot, plane, half):
+        number = {
+            (SIB, RE): 0,
+            (SIB, IM): half or 0,
+            (FAR, RE): 2,
+            (FAR, IM): 3,
+            (NEAR, RE): 4,
+            (NEAR, IM): 5 + (half or 0),
+            (BACK, RE): 7,
+            (BACK, IM): 8,
+        }[slot, plane]
+        return recv_sem.at[stage, number]
+
+    def remote(src, stage, slot, plane, half, group, device):
         return pltpu.make_async_remote_copy(
             src_ref=rows(src, half),
             dst_ref=rows(win.at[stage, slot, plane], half),
-            send_sem=send_sem.at[stage, number, part],
-            recv_sem=recv_sem.at[stage, slot, plane, part],
+            send_sem=send_sem.at[group],
+            recv_sem=flag(stage, slot, plane, half),
             device_id=(device,),
             device_id_type=MESH,
         )
 
-    def to_back_real(stage, own):
-        return [remote(own.at[RE], stage, FAR, RE, None, 0, partner[BACK])]
+    def to_back_real(stage, own, half):
+        return [remote(own.at[RE], stage, FAR, RE, half, TO_BACK, partner[BACK])]
 
     def to_back_imag(stage, own):
-        return [remote(own.at[IM], stage, NEAR, IM, 0, 1, partner[NEAR])]
+        return [remote(own.at[IM], stage, NEAR, IM, 0, TO_BACK, partner[NEAR])]
 
     def to_back_late(stage, other):
-        return [halfway(other, stage, BACK, 1, partner[NEAR])]
+        return [halfway(other, stage, BACK, TO_BACK, partner[NEAR])]
 
     def to_far_real(stage, own):
-        return [remote(own.at[RE], stage, BACK, RE, 0, 2, partner[FAR])]
+        return [remote(own.at[RE], stage, BACK, RE, 0, TO_FAR, partner[FAR])]
 
     def to_far_late(stage, own, other):
         return [
-            halfway(other, stage, NEAR, 3, partner[FAR]),
-            remote(own.at[RE], stage, BACK, RE, 1, 2, partner[FAR]),
-            remote(own.at[IM], stage, BACK, IM, 0, 3, partner[FAR]),
+            halfway(other, stage, NEAR, TO_FAR, partner[FAR]),
+            remote(own.at[RE], stage, BACK, RE, 1, TO_FAR, partner[FAR]),
+            remote(own.at[IM], stage, BACK, IM, 0, TO_FAR, partner[FAR]),
         ]
 
-    def halfway(other, stage, slot, number, device):
+    def halfway(other, stage, slot, group, device):
         return pltpu.make_async_remote_copy(
             src_ref=other,
             dst_ref=rows(win.at[stage, slot, IM], 1),
-            send_sem=send_sem.at[stage, number, 1],
-            recv_sem=recv_sem.at[stage, slot, IM, 1],
+            send_sem=send_sem.at[group],
+            recv_sem=flag(stage, slot, IM, 1),
             device_id=(device,),
             device_id_type=MESH,
         )
 
     def to_sibling(stage):
         return [
-            remote(ybuf.at[stage, IM], stage, SIB, IM, 1, 4, partner[SIB]),
-            remote(ybuf.at[stage, IM], stage, SIB, IM, 0, 4, partner[SIB]),
-            remote(ybuf.at[stage, RE], stage, SIB, RE, None, 5, partner[SIB]),
+            remote(ybuf.at[stage, IM], stage, SIB, IM, 1, TO_SIB, partner[SIB]),
+            remote(ybuf.at[stage, IM], stage, SIB, IM, 0, TO_SIB, partner[SIB]),
+            remote(ybuf.at[stage, RE], stage, SIB, RE, None, TO_SIB, partner[SIB]),
         ]
 
     def part_to_sibling(stage):
         return pltpu.make_async_remote_copy(
             src_ref=rows(zbuf.at[stage, IM], 1),
             dst_ref=zsib.at[stage],
-            send_sem=z_send.at[stage],
-            recv_sem=z_recv.at[stage],
+            send_sem=z_send,
+            recv_sem=z_recv.at[stage - 1],
             device_id=(partner[SIB],),
             device_id_type=MESH,
         )
@@ -196,10 +209,10 @@
         )
 
     def hand_real(stage):
-        return [remote(win.at[stage, FAR, RE], stage, NEAR, RE, None, 6, partner[SIB])]
+        return [remote(win.at[stage, FAR, RE], stage, NEAR, RE, None, TO_FAR, partner[SIB])]
 
     def hand_imag(stage, half):
-        return [remote(win.at[stage, NEAR, IM], stage, FAR, IM, half, 7, partner[SIB])]
+        return [remote(win.at[stage, NEAR, IM], stage, FAR, IM, half, TO_BACK, partner[SIB])]
 
     def start(copies):
         for copy in copies:
@@ -208,7 +221,8 @@
     def back_real(stage, own):
         @pl.when(has_back)
         def _():
-            start(to_back_real(stage, own))
+            start(to_back_real(stage, own, 0))
+            start(to_back_real(stage, own, 1))
 
     def far_real(stage, own):
         @pl.when(has_far)
@@ -222,8 +236,29 @@
 
     def arrived(stage, slot, plane, half=None):
         remote(
-            win.at[stage, slot, plane], stage, slot, plane, half, 0, partner[SIB]
+            win.at[stage, slot, plane], stage, slot, plane, half, TO_SIB, partner[SIB]
         ).wait_recv()
+
+    def arrived_rest(stage):
+        part = win.at[stage, SIB, :, pl.ds(0, M - HALF // 2)]
+        pltpu.make_async_remote_copy(
+            src_ref=part,
+            dst_ref=part,
+            send_sem=send_sem.at[TO_SIB],
+            recv_sem=flag(stage, SIB, RE, None),
+            device_id=(partner[SIB],),
+            device_id_type=MESH,
+        ).wait_recv()
+
+    def sent(ref, sem):
+        pltpu.make_async_remote_copy(
+            src_ref=ref,
+            dst_ref=ref,
+            send_sem=sem,
+            recv_sem=z_recv.at[0],
+            device_id=(partner[SIB],),
+            device_id_type=MESH,
+        ).wait_send()
 
     def late_far(stage, own, other):
         @pl.when(has_far)
@@ -447,28 +482,51 @@
             arrived(stage, NEAR, RE)
             take(stage, NEAR, RE)
             take(stage, NEAR, IM)
-            arrived(stage, BACK, RE, 0)
-            arrived(stage, BACK, RE, 1)
+            arrived(stage, BACK, RE)
             take(stage, BACK, RE)
 
         @pl.when(has_far)
         def _():
-            arrived(stage, FAR, IM, 1)
-            arrived(stage, FAR, IM, 0)
+            arrived(stage, FAR, IM)
             take(stage, FAR, IM)
 
+        after = stage + 1
+        more = stage < STAGES - 1
+
         @pl.when(has_back)
         def _():
-            arrived(stage, BACK, IM, 0)
-            arrived(stage, BACK, IM, 1)
+            arrived(stage, BACK, IM)
+
+        @pl.when(has_back & more)
+        def _():
+            high, low = split(received(stage, BACK, IM))
+            tall = jnp.concatenate([high, high, low], axis=0)
+            for half in (0, 1):
+                top = half * HALF
+                part = pl.ds(top, HALF)
+                left = jnp.dot(
+                    left_of[BACK, part], tall, preferred_element_type=F32
+                )
+                wide = [x[top : top + HALF] for x in (high, high, low)]
+                right = jnp.dot(
+                    jnp.concatenate(wide, axis=1),
+                    right_of[BACK, :, pl.ds(0, M)],
+                    preferred_element_type=F32,
+                )
+                slope = total[1, part] + (left - right)
+                total[1, part] = slope
+                ybuf[after, RE, part] = ybuf[0, RE, part] + ahead * slope
+                start(to_back_real(after, ybuf.at[after], half))
+                if half == 0:
+                    far_real(after, ybuf.at[after])
+
+        @pl.when(has_back & jnp.logical_not(more))
+        def _():
             take_real(stage, BACK, IM)
 
-        after = stage + 1
-
-        @pl.when(stage < STAGES - 1)
+        @pl.when(jnp.logical_not(has_back) & more)
         def _():
             ybuf[after, RE] = ybuf[0, RE] + ahead * total[1]
-            back_real(after, ybuf.at[after])
             far_real(after, ybuf.at[after])
 
         @pl.when(has_back & even)
@@ -483,9 +541,15 @@
             back_imag(after, ybuf.at[after])
             start(to_sibling(after))
 
-    def keep_part(after, ahead):
+    def keep_real(after, ahead):
         zbuf[after, RE] = ybuf[0, RE] + ahead * total[1]
+
+    def keep_imag(after, ahead):
         zbuf[after, IM] = ybuf[0, IM] - ahead * total[0]
+
+    def take_rest(stage, slot):
+        left, right = products(slot, received(stage, slot, IM), False, M)
+        total[0] -= left + right
 
     def below_even(stage, ahead):
         after = stage + 1
@@ -498,28 +562,32 @@
         arrived(stage, NEAR, RE)
         take_complex(stage, NEAR, RE)
         take_complex(stage, NEAR, IM)
-        arrived(stage, BACK, RE, 0)
-        arrived(stage, BACK, RE, 1)
+        arrived(stage, BACK, RE)
         take_complex(stage, BACK, RE)
-        arrived(stage, BACK, IM, 0)
-        arrived(stage, BACK, IM, 1)
-        take_complex(stage, BACK, IM)
+        arrived(stage, BACK, IM)
+        take_real(stage, BACK, IM)
 
         @pl.when(stage < STAGES - 1)
         def _():
-            keep_part(after, ahead)
+            keep_real(after, ahead)
             start(to_far_real(after, zbuf.at[after]))
+
+        take_rest(stage, BACK)
+
+        @pl.when(stage < STAGES - 1)
+        def _():
+            keep_imag(after, ahead)
             part_to_sibling(after).start()
 
         take_real(stage, FAR, RE)
-        arrived(stage, FAR, IM, 1)
-        arrived(stage, FAR, IM, 0)
+        arrived(stage, FAR, IM)
         take_real(stage, FAR, IM)
 
         @pl.when(stage < STAGES - 1)
         def _():
             ybuf[after, RE] = ybuf[0, RE] + ahead * total[1]
-            start(to_back_real(after, ybuf.at[after]))
+            start(to_back_real(after, ybuf.at[after], 0))
+            start(to_back_real(after, ybuf.at[after], 1))
             ybuf[after, IM] = ybuf[0, IM] - ahead * total[0]
             start(to_back_imag(after, ybuf.at[after]))
             start(to_sibling(after))
@@ -533,25 +601,29 @@
         start(hand_imag(stage, 1))
         arrived(stage, NEAR, IM, 0)
         start(hand_imag(stage, 0))
-        arrived(stage, FAR, IM, 1)
-        arrived(stage, FAR, IM, 0)
-        take_complex(stage, FAR, IM)
+        arrived(stage, FAR, IM)
+        take_real(stage, FAR, IM)
 
         @pl.when(stage < STAGES - 1)
         def _():
-            keep_part(after, ahead)
-            start(to_back_real(after, zbuf.at[after]))
+            keep_real(after, ahead)
+            start(to_back_real(after, zbuf.at[after], 0))
+            start(to_back_real(after, zbuf.at[after], 1))
+
+        take_rest(stage, FAR)
+
+        @pl.when(stage < STAGES - 1)
+        def _():
+            keep_imag(after, ahead)
             start(to_back_imag(after, zbuf.at[after]))
             part_to_sibling(after).start()
 
         take_real(stage, NEAR, IM)
         arrived(stage, NEAR, RE)
         take_real(stage, NEAR, RE)
-        arrived(stage, BACK, RE, 0)
-        arrived(stage, BACK, RE, 1)
+        arrived(stage, BACK, RE)
         take_real(stage, BACK, RE)
-        arrived(stage, BACK, IM, 0)
-        arrived(stage, BACK, IM, 1)
+        arrived(stage, BACK, IM)
         take_real(stage, BACK, IM)
 
         @pl.when(stage < STAGES - 1)
@@ -577,8 +649,7 @@
             start(to_back_late(stage, zsib.at[stage]))
 
     def stage_body(stage, carry):
-        arrived(stage, SIB, IM, 0)
-        arrived(stage, SIB, RE)
+        arrived_rest(stage)
         take(stage, SIB, RE)
         take(stage, SIB, IM)
 
@@ -622,37 +693,20 @@
     out[0, RE] = ybuf[0, RE] + (STEP / 6) * (acc[RE] + total[1])
     out[0, IM] = ybuf[0, IM] + (STEP / 6) * (acc[IM] - total[0])
 
-    def drain(stage, carry):
-        for copy in to_sibling(stage):
-            copy.wait_send()
-
-        @pl.when(has_back)
-        def _():
-            for copy in [
-                *to_back_real(stage, ybuf.at[stage]),
-                *to_back_imag(stage, ybuf.at[stage]),
-                *to_back_late(stage, zsib.at[stage]),
-                *hand_imag(stage, 0),
-                *hand_imag(stage, 1),
-            ]:
-                copy.wait_send()
-
-        @pl.when(has_far)
-        def _():
-            for copy in [
-                *to_far_real(stage, ybuf.at[stage]),
-                *to_far_late(stage, ybuf.at[stage], zsib.at[stage]),
-                *hand_real(stage),
-            ]:
-                copy.wait_send()
-
-        @pl.when(below & (stage > 0))
-        def _():
-            part_to_sibling(stage).wait_send()
-
-        return carry
-
-    lax.fori_loop(0, STAGES, drain, 0)
+    sent(ybuf, send_sem.at[TO_SIB])
+    most = win.at[pl.ds(0, 2), pl.ds(0, 3)]
+
+    @pl.when(has_back)
+    def _():
+        sent(most, send_sem.at[TO_BACK])
+
+    @pl.when(has_far)
+    def _():
+        sent(most, send_sem.at[TO_FAR])
+
+    @pl.when(below)
+    def _():
+        sent(zsib.at[pl.ds(0, STAGES - 1)], z_send)
 
     @pl.when(below & even)
     def _():
@@ -694,12 +748,12 @@
             pltpu.VMEM((3, 3 * M, M), BF),
             pltpu.VMEM((2, 2, 2, M, M), F32),
             pltpu.SemaphoreType.DMA((9,)),
-            pltpu.SemaphoreType.DMA((STAGES, 8, 2)),
-            pltpu.SemaphoreType.DMA((STAGES, 4, 2, 2)),
+            pltpu.SemaphoreType.DMA((3,)),
+            pltpu.SemaphoreType.DMA((STAGES, 9)),
             pltpu.SemaphoreType.DMA((2,)),
             pltpu.SemaphoreType.DMA((2,)),
-            pltpu.SemaphoreType.DMA((STAGES,)),
-            pltpu.SemaphoreType.DMA((STAGES,)),
+            pltpu.SemaphoreType.DMA,
+            pltpu.SemaphoreType.DMA((STAGES - 1,)),
         ],
         compiler_params=pltpu.CompilerParams(
             collective_id=0, has_side_effects=True, vmem_limit_bytes=48 << 20

time: 66.6 us -> 64.8 us (0.973)
  Pallas kernels: 65.7 us -> 63.9 us
    pallas_call x1, Pallas kernels: 65.7 us -> 63.9 us  [on_device(): pl.pallas_call(functools.partial(kernel, count), out_shape=jax.ShapeDtype...]
where the time goes in v3:
time: 64.8 us; the launch traced here: 64.7 us
  Pallas kernels  63.9 us (99%)
  local copies, waits for them, and re-layouts  0.8 us (1%)
    pallas_call x1, Pallas kernels, on_device(): pl.pallas_call(functools.partial(kernel, count), out_shape=jax.ShapeDtype...  63.9 us

profile of v3, /device:TPU:24, one launch (start us, length us, event | category | flops | bytes accessed | tf_op | source)
XLA Modules:
  0.0 64.7 jit_solution(16940754661538362196)
XLA Ops:
  0.0 63.9 %rk_step.1 = f32[1,2,256,256]{3,2,1,0:T(8,128)S(1)} custom-call(f32[2,3]{1,0:T(2,128)} %bath_hbm.1, f32[3]{0:T(128)} %damp_hbm.1, s32[1,3]{1,0:T(1,128)} %occ_hbm.1, s32[1,3]{1,0:T(1,128)} %up_hbm.1, s32[1,3]{1,0:T(1,128)} %down_hbm.1, f32[1,2,256,256]{3,2,1,0:T(8,128)} %state.1, f32[2,256,256]{2,1,0:T(8,128)} %h_static.1, f32[2,256,256]{2,1,0:T(8,128)} %drive_op.1, ...), custom_call_target="tpu_custom_call" | custom-call | tf_op jit(solution)/shard_map/rk_step/pallas_call | solution.py:725
  63.9 0.8 %copy.11 = f32[1,2,256,256]{3,2,1,0:T(8,128)} copy(f32[1,2,256,256]{3,2,1,0:T(8,128)S(1)} %rk_step.1) | data formatting | bytes 1048576

commit v4 on v3

--- a/solution.py
+++ b/solution.py
@@ -85,6 +85,7 @@
     below = (lax.rem(chip, ROW) == ROW - 1) & (chip < last)
     above = (lax.rem(chip, ROW) == 0) & (chip > 0)
     odd_one = jnp.logical_not(even)
+    across = (below & odd_one) | (above & even)
 
     moves = [
         (state.at[0], ybuf.at[0]),
@@ -112,18 +113,25 @@
 
     @pl.when(has_back)
     def _():
+        greet(BACK)
+
+    @pl.when(across)
+    def _():
         greet(NEAR)
-        greet(BACK)
 
     loads = [
-        pltpu.make_async_copy(src, dst, load_sem.at[i])
+        pltpu.make_async_copy(src, dst, load_sem.at[max(i, 3) - 3 if i else 6])
         for i, (src, dst) in enumerate(moves)
     ]
     for load in loads:
         load.start()
 
     pl.semaphore_wait(
-        barrier, 1 + jnp.where(has_far, 1, 0) + jnp.where(has_back, 2, 0)
+        barrier,
+        1
+        + jnp.where(has_far, 1, 0)
+        + jnp.where(has_back, 1, 0)
+        + jnp.where(across, 1, 0),
     )
 
     def rows(ref, half):
@@ -132,7 +140,7 @@
     def flag(stage, slot, plane, half):
         number = {
             (SIB, RE): 0,
-            (SIB, IM): half or 0,
+            (SIB, IM): 1,
             (FAR, RE): 2,
             (FAR, IM): 3,
             (NEAR, RE): 4,
@@ -155,42 +163,26 @@
     def to_back_real(stage, own, half):
         return [remote(own.at[RE], stage, FAR, RE, half, TO_BACK, partner[BACK])]
 
-    def to_back_imag(stage, own):
-        return [remote(own.at[IM], stage, NEAR, IM, 0, TO_BACK, partner[NEAR])]
-
-    def to_back_late(stage, other):
-        return [halfway(other, stage, BACK, TO_BACK, partner[NEAR])]
-
     def to_far_real(stage, own):
         return [remote(own.at[RE], stage, BACK, RE, 0, TO_FAR, partner[FAR])]
 
     def to_far_late(stage, own, other):
         return [
-            halfway(other, stage, NEAR, TO_FAR, partner[FAR]),
+            remote(other, stage, NEAR, IM, 1, TO_FAR, partner[FAR]),
+            remote(other, stage, NEAR, IM, 0, TO_FAR, partner[FAR]),
             remote(own.at[RE], stage, BACK, RE, 1, TO_FAR, partner[FAR]),
-            remote(own.at[IM], stage, BACK, IM, 0, TO_FAR, partner[FAR]),
+            remote(own.at[IM], stage, BACK, IM, None, TO_FAR, partner[FAR]),
         ]
-
-    def halfway(other, stage, slot, group, device):
-        return pltpu.make_async_remote_copy(
-            src_ref=other,
-            dst_ref=rows(win.at[stage, slot, IM], 1),
-            send_sem=send_sem.at[group],
-            recv_sem=flag(stage, slot, IM, 1),
-            device_id=(device,),
-            device_id_type=MESH,
-        )
 
     def to_sibling(stage):
         return [
-            remote(ybuf.at[stage, IM], stage, SIB, IM, 1, TO_SIB, partner[SIB]),
-            remote(ybuf.at[stage, IM], stage, SIB, IM, 0, TO_SIB, partner[SIB]),
+            remote(ybuf.at[stage, IM], stage, SIB, IM, None, TO_SIB, partner[SIB]),
             remote(ybuf.at[stage, RE], stage, SIB, RE, None, TO_SIB, partner[SIB]),
         ]
 
     def part_to_sibling(stage):
         return pltpu.make_async_remote_copy(
-            src_ref=rows(zbuf.at[stage, IM], 1),
+            src_ref=zbuf.at[stage, IM],
             dst_ref=zsib.at[stage],
             send_sem=z_send,
             recv_sem=z_recv.at[stage - 1],
@@ -229,25 +221,9 @@
         def _():
             start(to_far_real(stage, own))
 
-    def back_imag(stage, own):
-        @pl.when(has_back)
-        def _():
-            start(to_back_imag(stage, own))
-
     def arrived(stage, slot, plane, half=None):
         remote(
             win.at[stage, slot, plane], stage, slot, plane, half, TO_SIB, partner[SIB]
-        ).wait_recv()
-
-    def arrived_rest(stage):
-        part = win.at[stage, SIB, :, pl.ds(0, M - HALF // 2)]
-        pltpu.make_async_remote_copy(
-            src_ref=part,
-            dst_ref=part,
-            send_sem=send_sem.at[TO_SIB],
-            recv_sem=flag(stage, SIB, RE, None),
-            device_id=(partner[SIB],),
-            device_id_type=MESH,
         ).wait_recv()
 
     def sent(ref, sem):
@@ -265,21 +241,13 @@
         def _():
             start(to_far_late(stage, own, other))
 
-    def late_back(stage, other):
-        @pl.when(has_back)
-        def _():
-            start(to_back_late(stage, other))
-
     def send_late(stage):
-        arrived(stage, SIB, IM, 1)
-        other = rows(win.at[stage, SIB, IM], 1)
-        late_far(stage, ybuf.at[stage], other)
-        late_back(stage, other)
+        arrived(stage, SIB, IM)
+        late_far(stage, ybuf.at[stage], win.at[stage, SIB, IM])
 
     loads[0].wait()
     back_real(0, ybuf.at[0])
     far_real(0, ybuf.at[0])
-    back_imag(0, ybuf.at[0])
     start(to_sibling(0))
 
     @pl.when(below & even)
@@ -318,15 +286,17 @@
         )
         return left, right
 
-    def own_products(stage):
+    def own_products(stage, planes):
         slot = OWN + (stage + 1) // 2
         real, imag = ybuf[stage, RE], ybuf[stage, IM]
-        left, right = products(slot, real, True)
-        total[0] = rate * imag + (left[:M] - right[:, :M])
-        total[1] = (left[M:] + right[:, M:]) - rate * real
-        left, right = products(slot, imag, True)
-        total[0] -= left[M:] + right[:, M:]
-        total[1] += left[:M] - right[:, :M]
+        if RE in planes:
+            left, right = products(slot, real, True)
+            total[0] = rate * imag + (left[:M] - right[:, :M])
+            total[1] = (left[M:] + right[:, M:]) - rate * real
+        if IM in planes:
+            left, right = products(slot, imag, True)
+            total[0] -= left[M:] + right[:, M:]
+            total[1] += left[:M] - right[:, :M]
 
     def received(stage, slot, plane):
         value = win[stage, slot, plane]
@@ -407,18 +377,16 @@
     for k in range(MODES):
         rate = rate + occ[0, k].astype(F32) * damp[k]
 
-    loads[1].wait()
-    loads[2].wait()
+    pltpu.make_async_copy(raw, raw, load_sem.at[0]).wait()
     for k in range(2):
         value = raw[3 + 2 * k]
         herm[k, 0] = (value + value.T) * 0.5
         value = raw[4 + 2 * k]
         herm[k, 1] = (value - value.T) * 0.5
     put_own(0)
-    own_products(0)
+    own_products(0, (RE, IM))
     send_late(0)
 
-    loads[3].wait()
     for k in range(MODES):
         value = raw[k]
         raw[k] = (value + value.T) * 0.5
@@ -488,7 +456,7 @@
         @pl.when(has_far)
         def _():
             arrived(stage, FAR, IM)
-            take(stage, FAR, IM)
+            take_real(stage, FAR, IM)
 
         after = stage + 1
         more = stage < STAGES - 1
@@ -531,14 +499,15 @@
 
         @pl.when(has_back & even)
         def _():
-            value = received(stage, BACK, IM)
-            left, right = products(BACK, value, False, M)
-            total[0] -= left + right
+            take_rest(stage, BACK)
+
+        @pl.when(has_far & odd_one)
+        def _():
+            take_rest(stage, FAR)
 
         @pl.when(stage < STAGES - 1)
         def _():
             ybuf[after, IM] = ybuf[0, IM] - ahead * total[0]
-            back_imag(after, ybuf.at[after])
             start(to_sibling(after))
 
     def keep_real(after, ahead):
@@ -577,7 +546,6 @@
         @pl.when(stage < STAGES - 1)
         def _():
             keep_imag(after, ahead)
-            part_to_sibling(after).start()
 
         take_real(stage, FAR, RE)
         arrived(stage, FAR, IM)
@@ -589,7 +557,6 @@
             start(to_back_real(after, ybuf.at[after], 0))
             start(to_back_real(after, ybuf.at[after], 1))
             ybuf[after, IM] = ybuf[0, IM] - ahead * total[0]
-            start(to_back_imag(after, ybuf.at[after]))
             start(to_sibling(after))
 
     def below_odd(stage, ahead):
@@ -615,7 +582,6 @@
         @pl.when(stage < STAGES - 1)
         def _():
             keep_imag(after, ahead)
-            start(to_back_imag(after, zbuf.at[after]))
             part_to_sibling(after).start()
 
         take_real(stage, NEAR, IM)
@@ -634,22 +600,19 @@
             start(to_sibling(after))
 
     def late_below(stage):
-        arrived(stage, SIB, IM, 1)
-        part_to_sibling(stage).wait_recv()
-        other = rows(win.at[stage, SIB, IM], 1)
-
         @pl.when(even)
         def _():
+            part_to_sibling(stage).wait_recv()
             start(to_far_late(stage, zbuf.at[stage], zsib.at[stage]))
-            start(to_back_late(stage, other))
+            arrived(stage, SIB, IM)
 
         @pl.when(odd_one)
         def _():
-            start(to_far_late(stage, ybuf.at[stage], other))
-            start(to_back_late(stage, zsib.at[stage]))
+            arrived(stage, SIB, IM)
+            start(to_far_late(stage, ybuf.at[stage], win.at[stage, SIB, IM]))
 
     def stage_body(stage, carry):
-        arrived_rest(stage)
+        arrived(stage, SIB, RE)
         take(stage, SIB, RE)
         take(stage, SIB, IM)
 
@@ -676,7 +639,7 @@
             weight = jnp.where(stage == 0, 1.0, 2.0).astype(F32)
             acc[RE] += weight * total[1]
             acc[IM] -= weight * total[0]
-            own_products(stage + 1)
+            own_products(stage + 1, (RE,))
 
         @pl.when((stage < STAGES - 1) & jnp.logical_not(below))
         def _():
@@ -685,6 +648,10 @@
         @pl.when((stage < STAGES - 1) & below)
         def _():
             late_below(stage + 1)
+
+        @pl.when(stage < STAGES - 1)
+        def _():
+            own_products(stage + 1, (IM,))
 
         return carry
 
@@ -694,17 +661,16 @@
     out[0, IM] = ybuf[0, IM] + (STEP / 6) * (acc[IM] - total[0])
 
     sent(ybuf, send_sem.at[TO_SIB])
-    most = win.at[pl.ds(0, 2), pl.ds(0, 3)]
 
     @pl.when(has_back)
     def _():
-        sent(most, send_sem.at[TO_BACK])
+        sent(ybuf, send_sem.at[TO_BACK])
 
     @pl.when(has_far)
     def _():
-        sent(most, send_sem.at[TO_FAR])
-
-    @pl.when(below)
+        sent(win.at[pl.ds(0, 2)], send_sem.at[TO_FAR])
+
+    @pl.when(below & odd_one)
     def _():
         sent(zsib.at[pl.ds(0, STAGES - 1)], z_send)
 
@@ -743,11 +709,11 @@
             pltpu.VMEM((2, M, M), F32),
             pltpu.SMEM((2, 1, MODES), jnp.int32),
             pltpu.VMEM((STAGES, 2, M, M), F32),
-            pltpu.VMEM((STAGES, HALF, M), F32),
+            pltpu.VMEM((STAGES, M, M), F32),
             pltpu.VMEM((3, M, 3 * M), BF),
             pltpu.VMEM((3, 3 * M, M), BF),
             pltpu.VMEM((2, 2, 2, M, M), F32),
-            pltpu.SemaphoreType.DMA((9,)),
+            pltpu.SemaphoreType.DMA((7,)),
             pltpu.SemaphoreType.DMA((3,)),
             pltpu.SemaphoreType.DMA((STAGES, 9)),
             pltpu.SemaphoreType.DMA((2,)),

time: 64.8 us -> 63 us (0.972)
  Pallas kernels: 63.9 us -> 62.1 us
    pallas_call x1, Pallas kernels: 63.9 us -> 62.1 us  [on_device(): pl.pallas_call(functools.partial(kernel, count), out_shape=jax.ShapeDtype...]
where the time goes in v4:
time: 63 us; the launch traced here: 62.9 us
  Pallas kernels  62.1 us (99%)
  local copies, waits for them, and re-layouts  0.8 us (1%)
    pallas_call x1, Pallas kernels, on_device(): pl.pallas_call(functools.partial(kernel, count), out_shape=jax.ShapeDtype...  62.1 us

profile of v4, /device:TPU:24, one launch (start us, length us, event | category | flops | bytes accessed | tf_op | source)
XLA Modules:
  0.0 62.9 jit_solution(4550259509422286001)
XLA Ops:
  0.0 62.1 %rk_step.1 = f32[1,2,256,256]{3,2,1,0:T(8,128)S(1)} custom-call(f32[2,3]{1,0:T(2,128)} %bath_hbm.1, f32[3]{0:T(128)} %damp_hbm.1, s32[1,3]{1,0:T(1,128)} %occ_hbm.1, s32[1,3]{1,0:T(1,128)} %up_hbm.1, s32[1,3]{1,0:T(1,128)} %down_hbm.1, f32[1,2,256,256]{3,2,1,0:T(8,128)} %state.1, f32[2,256,256]{2,1,0:T(8,128)} %h_static.1, f32[2,256,256]{2,1,0:T(8,128)} %drive_op.1, ...), custom_call_target="tpu_custom_call" | custom-call | tf_op jit(solution)/shard_map/rk_step/pallas_call | solution.py:691
  62.1 0.8 %copy.11 = f32[1,2,256,256]{3,2,1,0:T(8,128)} copy(f32[1,2,256,256]{3,2,1,0:T(8,128)S(1)} %rk_step.1) | data formatting | bytes 1048576

commit v5 on v4

--- a/solution.py
+++ b/solution.py
@@ -146,7 +146,7 @@
             (NEAR, RE): 4,
             (NEAR, IM): 5 + (half or 0),
             (BACK, RE): 7,
-            (BACK, IM): 8,
+            (BACK, IM): 8 + (half or 0),
         }[slot, plane]
         return recv_sem.at[stage, number]
 
@@ -171,7 +171,8 @@
             remote(other, stage, NEAR, IM, 1, TO_FAR, partner[FAR]),
             remote(other, stage, NEAR, IM, 0, TO_FAR, partner[FAR]),
             remote(own.at[RE], stage, BACK, RE, 1, TO_FAR, partner[FAR]),
-            remote(own.at[IM], stage, BACK, IM, None, TO_FAR, partner[FAR]),
+            remote(own.at[IM], stage, BACK, IM, 0, TO_FAR, partner[FAR]),
+            remote(own.at[IM], stage, BACK, IM, 1, TO_FAR, partner[FAR]),
         ]
 
     def to_sibling(stage):
@@ -298,15 +299,15 @@
             total[0] -= left[M:] + right[:, M:]
             total[1] += left[:M] - right[:, :M]
 
-    def received(stage, slot, plane):
-        value = win[stage, slot, plane]
+    def received(stage, slot, plane, part=pl.ds(0, M)):
+        value = win[stage, slot, plane, part]
         if slot == SIB:
             return value
         who = odd_one if slot == FAR else even
         before = jnp.where(stage == STAGES - 1, STEP, STEP / 2).astype(F32)
         scale = jnp.where(above & who & (stage > 0), before, 0.0).astype(F32)
         which = 1 if slot == BACK else 0
-        other = extra[lax.rem(stage, 2), which, 1 - plane]
+        other = extra[lax.rem(stage, 2), which, 1 - plane, part]
         return value + (scale if plane == RE else -scale) * other
 
     def take_complex(stage, slot, plane):
@@ -461,47 +462,87 @@
         after = stage + 1
         more = stage < STAGES - 1
 
-        @pl.when(has_back)
-        def _():
-            arrived(stage, BACK, IM)
+        def piece(half, begin=0):
+            part = pl.ds(half * HALF, HALF)
+            high, low = split(received(stage, BACK, IM, part))
+            columns = [
+                left_of[BACK, pl.ds(begin, M), pl.ds(block * M + half * HALF, HALF)]
+                for block in range(3)
+            ]
+            return (
+                jnp.concatenate(columns, axis=1),
+                jnp.concatenate([high, high, low], axis=0),
+                jnp.concatenate([high, high, low], axis=1),
+                right_of[BACK, :, pl.ds(begin, M)],
+            )
+
+        def sides(half, begin):
+            p_part, tall, wide, p_all = piece(half, begin)
+            return (
+                jnp.dot(p_part, tall, preferred_element_type=F32),
+                jnp.dot(wide, p_all, preferred_element_type=F32),
+            )
+
+        top, bottom = pl.ds(0, HALF), pl.ds(HALF, HALF)
+
+        def next_real(part, half, slope):
+            total[1, part] = slope
+            ybuf[after, RE, part] = ybuf[0, RE, part] + ahead * slope
+            start(to_back_real(after, ybuf.at[after], half))
+            if half == 0:
+                far_real(after, ybuf.at[after])
 
         @pl.when(has_back & more)
         def _():
-            high, low = split(received(stage, BACK, IM))
-            tall = jnp.concatenate([high, high, low], axis=0)
-            for half in (0, 1):
-                top = half * HALF
-                part = pl.ds(top, HALF)
-                left = jnp.dot(
-                    left_of[BACK, part], tall, preferred_element_type=F32
-                )
-                wide = [x[top : top + HALF] for x in (high, high, low)]
-                right = jnp.dot(
-                    jnp.concatenate(wide, axis=1),
-                    right_of[BACK, :, pl.ds(0, M)],
-                    preferred_element_type=F32,
-                )
-                slope = total[1, part] + (left - right)
-                total[1, part] = slope
-                ybuf[after, RE, part] = ybuf[0, RE, part] + ahead * slope
-                start(to_back_real(after, ybuf.at[after], half))
-                if half == 0:
-                    far_real(after, ybuf.at[after])
-
-        @pl.when(has_back & jnp.logical_not(more))
-        def _():
-            take_real(stage, BACK, IM)
+            arrived(stage, BACK, IM, 0)
+            p_part, tall, wide, p_all = piece(0)
+            total[1] += jnp.dot(p_part, tall, preferred_element_type=F32)
+            total[1, top] -= jnp.dot(wide, p_all, preferred_element_type=F32)
+            arrived(stage, BACK, IM, 1)
+            p_part, tall, wide, p_all = piece(1)
+            left = jnp.dot(p_part[:HALF], tall, preferred_element_type=F32)
+            next_real(top, 0, total[1, top] + left)
+            left = jnp.dot(p_part[HALF:], tall, preferred_element_type=F32)
+            right = jnp.dot(wide, p_all, preferred_element_type=F32)
+            next_real(bottom, 1, total[1, bottom] + (left - right))
+
+        @pl.when(has_far & odd_one & jnp.logical_not(more))
+        def _():
+            take_rest(stage, FAR)
+
+        def finish(half, complex_too):
+            part = pl.ds(half * HALF, HALF)
+            left, right = sides(half, 0)
+            total[1] += left
+            total[1, part] -= right
+            if complex_too:
+                left, right = sides(half, M)
+                total[0] -= left
+                total[0, part] -= right
+
+        for half in (0, 1):
+            @pl.when(has_back & jnp.logical_not(more))
+            def _():
+                arrived(stage, BACK, IM, half)
+
+            @pl.when(has_back & even & jnp.logical_not(more))
+            def _():
+                finish(half, True)
+
+            @pl.when(has_back & odd_one & jnp.logical_not(more))
+            def _():
+                finish(half, False)
 
         @pl.when(jnp.logical_not(has_back) & more)
         def _():
             ybuf[after, RE] = ybuf[0, RE] + ahead * total[1]
             far_real(after, ybuf.at[after])
 
-        @pl.when(has_back & even)
+        @pl.when(has_back & even & more)
         def _():
             take_rest(stage, BACK)
 
-        @pl.when(has_far & odd_one)
+        @pl.when(has_far & odd_one & more)
         def _():
             take_rest(stage, FAR)
 
@@ -533,7 +574,8 @@
         take_complex(stage, NEAR, IM)
         arrived(stage, BACK, RE)
         take_complex(stage, BACK, RE)
-        arrived(stage, BACK, IM)
+        arrived(stage, BACK, IM, 0)
+        arrived(stage, BACK, IM, 1)
         take_real(stage, BACK, IM)
 
         @pl.when(stage < STAGES - 1)
@@ -589,7 +631,8 @@
         take_real(stage, NEAR, RE)
         arrived(stage, BACK, RE)
         take_real(stage, BACK, RE)
-        arrived(stage, BACK, IM)
+        arrived(stage, BACK, IM, 0)
+        arrived(stage, BACK, IM, 1)
         take_real(stage, BACK, IM)
 
         @pl.when(stage < STAGES - 1)
@@ -715,7 +758,7 @@
             pltpu.VMEM((2, 2, 2, M, M), F32),
             pltpu.SemaphoreType.DMA((7,)),
             pltpu.SemaphoreType.DMA((3,)),
-            pltpu.SemaphoreType.DMA((STAGES, 9)),
+            pltpu.SemaphoreType.DMA((STAGES, 10)),
             pltpu.SemaphoreType.DMA((2,)),
             pltpu.SemaphoreType.DMA((2,)),
             pltpu.SemaphoreType.DMA,

time: 63 us -> 62.7 us (level)
  no operation moved by 1% of the time
where the time goes in v5:
time: 62.7 us; the launch traced here: 62.6 us
  Pallas kernels  61.8 us (99%)
  local copies, waits for them, and re-layouts  0.8 us (1%)
    pallas_call x1, Pallas kernels, on_device(): pl.pallas_call(functools.partial(kernel, count), out_shape=jax.ShapeDtype...  61.8 us

profile of v5, /device:TPU:24, one launch (start us, length us, event | category | flops | bytes accessed | tf_op | source)
XLA Modules:
  0.0 62.6 jit_solution(6758629147594130845)
XLA Ops:
  0.0 61.8 %rk_step.1 = f32[1,2,256,256]{3,2,1,0:T(8,128)S(1)} custom-call(f32[2,3]{1,0:T(2,128)} %bath_hbm.1, f32[3]{0:T(128)} %damp_hbm.1, s32[1,3]{1,0:T(1,128)} %occ_hbm.1, s32[1,3]{1,0:T(1,128)} %up_hbm.1, s32[1,3]{1,0:T(1,128)} %down_hbm.1, f32[1,2,256,256]{3,2,1,0:T(8,128)} %state.1, f32[2,256,256]{2,1,0:T(8,128)} %h_static.1, f32[2,256,256]{2,1,0:T(8,128)} %drive_op.1, ...), custom_call_target="tpu_custom_call" | custom-call | tf_op jit(solution)/shard_map/rk_step/pallas_call | solution.py:734
  61.8 0.8 %copy.11 = f32[1,2,256,256]{3,2,1,0:T(8,128)} copy(f32[1,2,256,256]{3,2,1,0:T(8,128)S(1)} %rk_step.1) | data formatting | bytes 1048576

commit v6 on v5

--- a/solution.py
+++ b/solution.py
@@ -63,6 +63,7 @@
     load_sem,
     send_sem,
     recv_sem,
+    sib_recv,
     rim_send,
     rim_recv,
     z_send,
@@ -148,7 +149,9 @@
             (BACK, RE): 7,
             (BACK, IM): 8 + (half or 0),
         }[slot, plane]
-        return recv_sem.at[stage, number]
+        if slot == SIB:
+            return sib_recv.at[lax.rem(stage, 2), number]
+        return recv_sem.at[lax.rem(stage, 3), number - 2]
 
     def remote(src, stage, slot, plane, half, group, device):
         return pltpu.make_async_remote_copy(
@@ -758,7 +761,8 @@
             pltpu.VMEM((2, 2, 2, M, M), F32),
             pltpu.SemaphoreType.DMA((7,)),
             pltpu.SemaphoreType.DMA((3,)),
-            pltpu.SemaphoreType.DMA((STAGES, 10)),
+            pltpu.SemaphoreType.DMA((3, 8)),
+            pltpu.SemaphoreType.DMA((2, 2)),
             pltpu.SemaphoreType.DMA((2,)),
             pltpu.SemaphoreType.DMA((2,)),
             pltpu.SemaphoreType.DMA,

time: 62.7 us -> 62.6 us (level)
  no operation moved by 1% of the time
where the time goes in v6:
time: 62.6 us; the launch traced here: 62.5 us
  Pallas kernels  61.7 us (99%)
  local copies, waits for them, and re-layouts  0.8 us (1%)
    pallas_call x1, Pallas kernels, on_device(): pl.pallas_call(functools.partial(kernel, count), out_shape=jax.ShapeDtype...  61.7 us

profile of v6, /device:TPU:24, one launch (start us, length us, event | category | flops | bytes accessed | tf_op | source)
XLA Modules:
  0.0 62.5 jit_solution(5796433925183424904)
XLA Ops:
  0.0 61.7 %rk_step.1 = f32[1,2,256,256]{3,2,1,0:T(8,128)S(1)} custom-call(f32[2,3]{1,0:T(2,128)} %bath_hbm.1, f32[3]{0:T(128)} %damp_hbm.1, s32[1,3]{1,0:T(1,128)} %occ_hbm.1, s32[1,3]{1,0:T(1,128)} %up_hbm.1, s32[1,3]{1,0:T(1,128)} %down_hbm.1, f32[1,2,256,256]{3,2,1,0:T(8,128)} %state.1, f32[2,256,256]{2,1,0:T(8,128)} %h_static.1, f32[2,256,256]{2,1,0:T(8,128)} %drive_op.1, ...), custom_call_target="tpu_custom_call" | custom-call | tf_op jit(solution)/shard_map/rk_step/pallas_call | solution.py:737
  61.7 0.8 %copy.11 = f32[1,2,256,256]{3,2,1,0:T(8,128)} copy(f32[1,2,256,256]{3,2,1,0:T(8,128)S(1)} %rk_step.1) | data formatting | bytes 1048576

commit v7 on v6

--- a/solution.py
+++ b/solution.py
@@ -142,7 +142,7 @@
         number = {
             (SIB, RE): 0,
             (SIB, IM): 1,
-            (FAR, RE): 2,
+            (FAR, RE): 2 if half == 1 else 10,
             (FAR, IM): 3,
             (NEAR, RE): 4,
             (NEAR, IM): 5 + (half or 0),
@@ -204,8 +204,8 @@
             device_id_type=MESH,
         )
 
-    def hand_real(stage):
-        return [remote(win.at[stage, FAR, RE], stage, NEAR, RE, None, TO_FAR, partner[SIB])]
+    def hand_real(stage, half):
+        return [remote(win.at[stage, FAR, RE], stage, NEAR, RE, half, TO_FAR, partner[SIB])]
 
     def hand_imag(stage, half):
         return [remote(win.at[stage, NEAR, IM], stage, FAR, IM, half, TO_BACK, partner[SIB])]
@@ -435,8 +435,10 @@
     def usual(stage, ahead):
         @pl.when(has_far)
         def _():
-            arrived(stage, FAR, RE)
-            start(hand_real(stage))
+            arrived(stage, FAR, RE, 0)
+            start(hand_real(stage, 0))
+            arrived(stage, FAR, RE, 1)
+            start(hand_real(stage, 1))
 
         @pl.when(has_back)
         def _():
@@ -568,8 +570,10 @@
         after = stage + 1
         arrived(stage, NEAR, IM, 1)
         start(hand_imag(stage, 1))
-        arrived(stage, FAR, RE)
-        start(hand_real(stage))
+        arrived(stage, FAR, RE, 0)
+        start(hand_real(stage, 0))
+        arrived(stage, FAR, RE, 1)
+        start(hand_real(stage, 1))
         arrived(stage, NEAR, IM, 0)
         start(hand_imag(stage, 0))
         arrived(stage, NEAR, RE)
@@ -606,8 +610,10 @@
 
     def below_odd(stage, ahead):
         after = stage + 1
-        arrived(stage, FAR, RE)
-        start(hand_real(stage))
+        arrived(stage, FAR, RE, 0)
+        start(hand_real(stage, 0))
+        arrived(stage, FAR, RE, 1)
+        start(hand_real(stage, 1))
         take_complex(stage, FAR, RE)
         arrived(stage, NEAR, IM, 1)
         start(hand_imag(stage, 1))
@@ -761,7 +767,7 @@
             pltpu.VMEM((2, 2, 2, M, M), F32),
             pltpu.SemaphoreType.DMA((7,)),
             pltpu.SemaphoreType.DMA((3,)),
-            pltpu.SemaphoreType.DMA((3, 8)),
+            pltpu.SemaphoreType.DMA((3, 9)),
             pltpu.SemaphoreType.DMA((2, 2)),
             pltpu.SemaphoreType.DMA((2,)),
             pltpu.SemaphoreType.DMA((2,)),

time: 62.6 us -> 62.6 us (level)
  no operation moved by 1% of the time
where the time goes in v7:
time: 62.6 us; the launch traced here: 62.5 us
  Pallas kernels  61.7 us (99%)
  local copies, waits for them, and re-layouts  0.8 us (1%)
    pallas_call x1, Pallas kernels, on_device(): pl.pallas_call(functools.partial(kernel, count), out_shape=jax.ShapeDtype...  61.7 us

profile of v7, /device:TPU:24, one launch (start us, length us, event | category | flops | bytes accessed | tf_op | source)
XLA Modules:
  0.0 62.5 jit_solution(2818253757021982891)
XLA Ops:
  0.0 61.7 %rk_step.1 = f32[1,2,256,256]{3,2,1,0:T(8,128)S(1)} custom-call(f32[2,3]{1,0:T(2,128)} %bath_hbm.1, f32[3]{0:T(128)} %damp_hbm.1, s32[1,3]{1,0:T(1,128)} %occ_hbm.1, s32[1,3]{1,0:T(1,128)} %up_hbm.1, s32[1,3]{1,0:T(1,128)} %down_hbm.1, f32[1,2,256,256]{3,2,1,0:T(8,128)} %state.1, f32[2,256,256]{2,1,0:T(8,128)} %h_static.1, f32[2,256,256]{2,1,0:T(8,128)} %drive_op.1, ...), custom_call_target="tpu_custom_call" | custom-call | tf_op jit(solution)/shard_map/rk_step/pallas_call | solution.py:743
  61.7 0.8 %copy.11 = f32[1,2,256,256]{3,2,1,0:T(8,128)} copy(f32[1,2,256,256]{3,2,1,0:T(8,128)S(1)} %rk_step.1) | data formatting | bytes 1048576
